TPU v7x, 256 devices: a whole 4x4x8 slice. The times are simulated.
256 devices in a mesh: dp: 8 (over z), expert: 32 (over x, y, core).
Axes of the slice: x: 4, y: 4, z: 8, core: 2. Of those that a mesh axis runs over, the one named last changes fastest.
Arguments:
- tokens: bfloat16 [256, 212, 1024], P(('dp', 'expert')), may hold values from -6 to 6
- expert_ids: int32 [256, 212, 1], P(('dp', 'expert')), may hold values from 0 to 31; in each aligned block of 212 rows (0 to 211, 212 to 423, ..., all dimensions but the last counted through in order) at most 9 rows name the same one
- caption_lengths: int32 [256], P(('dp', 'expert')), may hold values from 1 to 16, as said below
- layer_norm_gain: float32 [1024], replicated, may hold values from 0.5 to 1.5
- router: float32 [1024, 32], replicated, may hold values from -0.1875 to 0.1875
- w_up: bfloat16 [32, 1024, 4096], P('expert', None, 'dp'), may hold values from -0.1875 to 0.1875
- w_down: bfloat16 [32, 4096, 1024], P('expert', 'dp'), may hold values from -0.09375 to 0.09375
- logit_scale: float32 [1], replicated, may hold values from 5 to 20
- logit_bias: float32 [1], replicated, may hold values from -4 to -1.5
Outputs:
- loss: float32 [1], replicated
- grad_tokens: bfloat16 [256, 212, 1024], P(('dp', 'expert'))
- grad_up: float32 [32, 1024, 4096], P('expert', None, 'dp')
- grad_down: float32 [32, 4096, 1024], P('expert', 'dp')
- grad_router: float32 [1024, 32], replicated
- layer_gain_gradient: float32 [1024], replicated
Inputs may be any that keep to these rules, and one draw needn't show every extreme that they name: `expert_ids`: among the rows of one device (aligned blocks of 212 rows, devices ordered by dp then expert) no expert is named more than 9 times, a bound that some block reaches. `caption_lengths`: some caption has all 16 tokens.
All inputs are finite; a program needn't handle non-finite values.
Results may differ from a plain program's by a relative error of at most 0.009.
Values may be sent and summed in bfloat16 or wider, within the bound.
No kernel may reach another device: no remote copies, remote signals or barrier semaphores. Data moves between devices by JAX's collectives and lax.ppermute only.
A program may use at most 128 MiB of HBM per device.

v0:
```python
import jax
import jax.numpy as jnp
from jax import lax
from jax.sharding import PartitionSpec as P

D = 1024
PATCH = 196
CAPLEN = 16
SEQ = 212


eps = 1e-06
loss_scale = 1024.0


def gelu_slope(pre):
    return (
        0.5 * (1.0 + lax.erf(pre * 0.7071067811865476))
        + pre * jnp.exp(-0.5 * pre * pre) * 0.3989422804014327
    )


def deliver(buffer, experts, slots):
    width = buffer.shape[-1]
    sent = lax.all_to_all(
        buffer.reshape(experts, 1, slots, width), "expert", split_axis=0, concat_axis=1, tiled=True
    )
    shaped = sent.reshape(sent.shape[0], 1, sent.shape[1], slots, width)
    whole = lax.all_gather(shaped, "dp", axis=1, tiled=True)
    return whole.reshape(whole.shape[0], -1, width)


def give_back(partial_value, n_dp, n_expert, slots):
    local = partial_value.shape[0]
    width = partial_value.shape[-1]
    summed = lax.psum_scatter(
        partial_value.reshape(local, n_dp, n_expert * slots, width).astype(jnp.bfloat16),
        "dp",
        scatter_dimension=1,
        tiled=True,
    )
    rounded = summed.reshape(local, n_expert, slots, width)
    returned = lax.all_to_all(rounded, "expert", split_axis=1, concat_axis=0, tiled=True)
    return returned.reshape(-1, width)


def body(
    tokens,
    expert_ids,
    caption_lengths,
    layer_norm_gain,
    router,
    w_up,
    w_down,
    logit_scale,
    logit_bias,
):
    n_dp = lax.axis_size("dp")
    n_expert = lax.axis_size("expert")
    pair_dev = tokens.shape[0]
    rows = pair_dev * SEQ
    experts = router.shape[1]
    slots = rows * 4 // (3 * experts) + 1
    pairs_all = pair_dev * n_dp * n_expert
    input_rows = tokens.reshape(rows, D).astype(jnp.float32)
    input_mean = jnp.mean(input_rows, axis=1, keepdims=True)
    var_x = jnp.mean((input_rows - input_mean) ** 2, axis=1, keepdims=True)
    inverse_deviation = 1.0 / jnp.sqrt(var_x + eps)
    centered_scaled_input = (input_rows - input_mean) * inverse_deviation
    normalized_input = (centered_scaled_input * layer_norm_gain).astype(jnp.bfloat16)
    ids = expert_ids.reshape(rows)
    onehot = (ids[:, None] == jnp.arange(experts, dtype=jnp.int32)[None, :]).astype(jnp.int32)
    slot = jnp.sum((jnp.cumsum(onehot, axis=0) - 1) * onehot, axis=1)
    dest = ids * slots + slot
    onehot_f = onehot.astype(jnp.float32)
    buffer = jnp.zeros((experts * slots, D), jnp.bfloat16).at[dest].set(normalized_input)
    gathered = deliver(buffer, experts, slots)
    pre = jnp.einsum("erd,edf->erf", gathered, w_up, preferred_element_type=jnp.float32)
    act = jax.nn.gelu(pre, approximate=False).astype(jnp.bfloat16)
    partial_value = jnp.einsum("erf,efd->erd", act, w_down, preferred_element_type=jnp.float32)
    moe = give_back(partial_value, n_dp, n_expert, slots)[dest].astype(jnp.float32)
    xnf = normalized_input.astype(jnp.float32)
    router_logits = jnp.dot(xnf, router, precision=lax.Precision.HIGHEST)
    gate = jax.nn.sigmoid(jnp.sum(router_logits * onehot_f, axis=1))
    y = (input_rows + gate[:, None] * moe).reshape(pair_dev, SEQ, D)
    img = jnp.mean(y[:, :PATCH], axis=1)
    lengths = caption_lengths.astype(jnp.float32)
    mask = (jnp.arange(CAPLEN, dtype=jnp.int32)[None, :] < caption_lengths[:, None]).astype(
        jnp.float32
    )
    txt = jnp.sum(y[:, PATCH:] * mask[:, :, None], axis=1) / lengths[:, None]
    ru = jnp.sqrt(jnp.mean(img * img, axis=1, keepdims=True) + eps)
    rv = jnp.sqrt(jnp.mean(txt * txt, axis=1, keepdims=True) + eps)
    u = img / ru
    v = txt / rv
    scale = logit_scale[0]
    first = lax.axis_index(("dp", "expert")) * pair_dev
    mine = first + jnp.arange(pair_dev, dtype=jnp.int32)
    every = jnp.arange(pairs_all, dtype=jnp.int32)
    own_sign = jnp.where(mine[:, None] == every[None, :], 1.0, -1.0)
    v_all = lax.all_gather(v, ("dp", "expert"), axis=0, tiled=True)
    logits = scale * jnp.dot(u, v_all.T, precision=lax.Precision.HIGHEST) / D + logit_bias[0]
    loss_term = -jnp.sum(jax.nn.log_sigmoid(own_sign * logits)) / pairs_all
    coef = -(loss_scale / pairs_all) * own_sign * jax.nn.sigmoid(-own_sign * logits)
    du = scale / D * jnp.dot(coef, v_all, precision=lax.Precision.HIGHEST)
    dv_terms = scale / D * jnp.dot(coef.T, u, precision=lax.Precision.HIGHEST)
    dv = lax.psum_scatter(dv_terms, ("dp", "expert"), scatter_dimension=0, tiled=True)
    dimg = (du - u * jnp.mean(du * u, axis=1, keepdims=True)) / ru
    dtxt = (dv - v * jnp.mean(dv * v, axis=1, keepdims=True)) / rv
    dy_img = jnp.broadcast_to(dimg[:, None, :] / PATCH, (pair_dev, PATCH, D))
    dy_txt = (dtxt / lengths[:, None])[:, None, :] * mask[:, :, None]
    dy = jnp.concatenate([dy_img, dy_txt], axis=1).reshape(rows, D)
    dmoe = (gate[:, None] * dy).astype(jnp.bfloat16)
    dgl = jnp.sum(dy * moe, axis=1) * gate * (1.0 - gate)
    router_part = jnp.dot(xnf.T, onehot_f * dgl[:, None], precision=lax.Precision.HIGHEST)
    grad_buffer = jnp.zeros((experts * slots, D), jnp.bfloat16).at[dest].set(dmoe)
    gathered_grads = deliver(grad_buffer, experts, slots)
    dact = jnp.einsum("erd,efd->erf", gathered_grads, w_down, preferred_element_type=jnp.float32)
    dpre = (dact * gelu_slope(pre)).astype(jnp.bfloat16)
    grad_down = jnp.einsum("erf,erd->efd", act, gathered_grads, preferred_element_type=jnp.float32)
    grad_up = jnp.einsum("erd,erf->edf", gathered, dpre, preferred_element_type=jnp.float32)
    back_partial = jnp.einsum("erf,edf->erd", dpre, w_up, preferred_element_type=jnp.float32)
    dxe = give_back(back_partial, n_dp, n_expert, slots)[dest].astype(jnp.float32)
    router_rows = jnp.dot(onehot_f, router.T, precision=lax.Precision.HIGHEST)
    gradient_normalized_input = dxe + dgl[:, None] * router_rows
    gain_partial_term = jnp.sum(gradient_normalized_input * centered_scaled_input, axis=0)
    scaled_output_gradient = gradient_normalized_input * layer_norm_gain
    normed_input_gradient = (
        scaled_output_gradient
        - jnp.mean(scaled_output_gradient, axis=1, keepdims=True)
        - centered_scaled_input
        * jnp.mean(scaled_output_gradient * centered_scaled_input, axis=1, keepdims=True)
    ) * inverse_deviation
    grad_tokens = (dy + normed_input_gradient).astype(jnp.bfloat16).reshape(pair_dev, SEQ, D)
    loss, grad_router, layer_gain_gradient = lax.psum(
        (loss_term, router_part, gain_partial_term), ("dp", "expert")
    )
    return (loss.reshape(1), grad_tokens, grad_up, grad_down, grad_router, layer_gain_gradient)


def solution(mesh):
    return jax.shard_map(
        body,
        mesh=mesh,
        in_specs=(
            P(("dp", "expert"), None, None),
            P(("dp", "expert"), None, None),
            P(("dp", "expert")),
            P(),
            P(),
            P("expert", None, "dp"),
            P("expert", "dp", None),
            P(),
            P(),
        ),
        out_specs=(
            P(),
            P(("dp", "expert"), None, None),
            P("expert", None, "dp"),
            P("expert", "dp", None),
            P(),
            P(),
        ),
        check_vma=False,
    )
```

profile of v0, /device:TPU:1, one launch (start us, length us, event | category | flops | bytes accessed | tf_op | source)
XLA Modules:
  0.0 1022.5 jit_solution(2046483523152713916)
XLA Ops:
  7.2 1.2 convert_reduce_fusion
  8.5 1.3 fusion.38
  12.8 2.3 scatter_custom_fusion
  15.4 25.3 %all_to_all.16 = bf16[32,1,9,1024]{3,2,1,0:T(8,128)(2,1)S(1)} all-to-all(bf16[32,1,9,1024]{3,2,1,0:T(8,128)(2,1)S(1)} %bitcast.149), channel_id=1, replica_groups=mesh['dp'=8,'expert'=32] {'expert'}, dimensions={0} | all-to-all | bytes 1179648 | tf_op jit(solution)/shard_map/all_to_all | solution.py:25
  40.7 1.2 copy.21
  42.1 58.8 %all-gather.7.cloned.1.call-done = bf16[256,1,9,1024]{3,0,2,1:T(8,128)(2,1)} async-done(((bf16[32,1,9,1024]{3,0,2,1:T(8,128)(2,1)}), bf16[256,1,9,1024]{3,0,2,1:T(8,128)(2,1)}) %all-gather.7.cloned.1.call-update) | async-done | bytes 4718608 | tf_op jit(solution)/shard_map/all_gather | solution.py:29
  100.9 8.7 copy.22
  109.6 9.8 reshape.491
  119.5 14.9 %fusion.2 = (bf16[2304,512]{1,0:T(8,128)(2,1)S(1)}, f32[2304,512]{1,0:T(8,128)}) fusion(bf16[2304,1024]{1,0:T(8,128)(2,1)} %reshape.491, bf16[1,1024,512]{2,1,0:T(8,128)(2,1)S(1)} %copy-done), kind=kOutput, calls=%fused_computation.9 | convolution fusion | flops 2492596224 | bytes 12845056 | tf_op jit(solution)/shard_map/erd,edf->erf/dot_general | solution.py:78
  134.4 1.4 copy-done.27
  135.8 4.2 convert_bitcast_fusion.1
  140.8 58.3 %reduce-scatter.3.cloned.1.call-done = bf16[1,1,288,1024]{3,2,1,0:T(8,128)(2,1)} async-done(((bf16[1,8,288,1024]{3,2,1,0:T(8,128)(2,1)}), bf16[1,1,288,1024]{3,2,1,0:T(8,128)(2,1)}) %reduce-scatter.3.cloned.1.call-update) | async-done | bytes 589840 | tf_op jit(solution)/shard_map/reduce_scatter | solution.py:36
  199.1 2.2 reshape.494
  201.2 7.5 all-to-all-start.1
  209.8 15.8 %all-to-all-done.1 = bf16[1,32,9,1024]{3,2,0,1:T(8,128)(2,1)S(1)} async-done(((bf16[1,32,9,1024]{3,2,0,1:T(8,128)(2,1)}), bf16[1,32,9,1024]{3,2,0,1:T(8,128)(2,1)S(1)}, u32[]{:S(2)}, u32[]{:S(2)}) %all-to-all-start.1) | async-done | bytes 589856 | tf_op jit(solution)/shard_map/all_to_all | solution.py:43
  225.9 1.1 gather_fusion
  232.2 94.7 %all-gather.9.cloned.1.call-done = f32[262144]{0:T(1024)} async-done(((f32[1024]{0:T(1024)}), f32[262144]{0:T(1024)}) %all-gather.9.cloned.1.call-update) | async-done | bytes 1048592 | tf_op jit(solution)/shard_map/all_gather | solution.py:101
  326.9 1.4 reshape.539
  328.2 0.9 fusion.61
  329.1 0.7 divide_multiply_fusion.1
  329.9 1.1 multiply_multiply_fusion.6
  333.0 252.8 %all-reduce.8.cloned.1.call-done = f32[256,1024]{1,0:T(8,128)} async-done(((f32[256,1024]{1,0:T(8,128)}), f32[256,1024]{1,0:T(8,128)}) %all-reduce.8.cloned.1.call-update) | async-done | bytes 1048592
  585.7 1.4 multiply_reduce_fusion.1
  587.7 0.8 subtract_divide_fusion
  588.7 2.5 scatter_custom_fusion.1
  591.2 1.3 reshape.498
  592.5 25.2 %all_to_all.17 = bf16[32,1,9,1024]{3,2,1,0:T(8,128)(2,1)S(1)} all-to-all(bf16[32,1,9,1024]{3,2,1,0:T(8,128)(2,1)S(1)} %bitcast.150), channel_id=1, replica_groups=mesh['dp'=8,'expert'=32] {'expert'}, dimensions={0} | all-to-all | bytes 1179648 | tf_op jit(solution)/shard_map/all_to_all | solution.py:25
  617.7 1.2 copy.25
  619.0 55.5 %all-gather.11.cloned.1.call-done = bf16[256,1,9,1024]{3,0,2,1:T(8,128)(2,1)} async-done(((bf16[32,1,9,1024]{3,0,2,1:T(8,128)(2,1)}), bf16[256,1,9,1024]{3,0,2,1:T(8,128)(2,1)}) %all-gather.11.cloned.1.call-update) | async-done | bytes 4718608 | tf_op jit(solution)/shard_map/all_gather | solution.py:29
  674.5 8.7 copy.26
  683.2 9.9 reshape.500
  693.2 7.0 fusion.14
  700.1 1.4 copy-done.6
  701.6 4.4 convert_bitcast_fusion
  707.2 1.0 fusion.51
  708.2 7.0 convolution_bitcast_fusion
  715.2 49.9 %reduce-scatter.5.cloned.1.call-done = bf16[1,1,288,1024]{3,2,1,0:T(8,128)(2,1)} async-done(((bf16[1,8,288,1024]{3,2,1,0:T(8,128)(2,1)}), bf16[1,1,288,1024]{3,2,1,0:T(8,128)(2,1)}) %reduce-scatter.5.cloned.1.call-update) | async-done | bytes 589840 | tf_op jit(solution)/shard_map/reduce_scatter | solution.py:36
  765.1 2.2 reshape.501
  767.2 7.5 all-to-all-start.3
  774.8 7.1 convolution_bitcast_fusion.1
  781.9 10.0 all-to-all-done.3
  791.8 1.4 reshape.502
  793.3 2.0 gather_fusion.1
  795.2 2.3 fusion.37
  797.6 1.1 fusion.44
  798.7 74.7 %all-reduce.2 = (f32[1]{0:T(128)}, f32[1024]{0:T(1024)}) all-reduce(f32[1]{0:T(128)} %bitcast.20, f32[1024]{0:T(1024)S(1)} %get-tuple-element.6), channel_id=1, replica_groups=mesh['dp'=8,'expert'=32] {'dp','expert'}, use_global_device_ids=true, to_apply=%region_13.14 | all-reduce | flops 1025 | bytes 8200 | tf_op jit(solution)/shard_map/psum | solution.py:135
  873.5 140.6 %all-reduce.6.cloned.1.call-done = f32[1024,32]{0,1:T(8,128)} async-done(((f32[1024,32]{0,1:T(8,128)}), f32[1024,32]{0,1:T(8,128)}) %all-reduce.6.cloned.1.call-update) | async-done | bytes 131088 | tf_op jit(solution)/shard_map/psum | solution.py:135
  1014.1 1.6 copy.37
  (101 shorter events, 9.4 us)
Async XLA Ops:
  7.2 112.3 %copy-start = (bf16[1,1024,512]{2,1,0:T(8,128)(2,1)S(1)}, bf16[1,1024,512]{2,1,0:T(8,128)(2,1)}, u32[]{:S(2)}) copy-start(bf16[1,1024,512]{2,1,0:T(8,128)(2,1)} %param.14) | copy-start | bytes 3145732
  7.2 93.7 %all-gather.7.cloned.1.call-start = ((), (), s32[]{:S(2)}) async-start(), calls=%async_computation.9 | async-start | bytes 5308416 | tf_op jit(solution)/shard_map/all_gather | solution.py:29
  8.5 200.3 %copy-start.11 = (f32[212]{0:T(256)}, f32[212]{0:T(256)S(1)}, u32[]{:S(2)}) copy-start(f32[212]{0:T(256)S(1)} %broadcast_multiply_fusion.3) | copy-start | bytes 2548
  9.8 199.0 %copy-start.15 = (f32[212]{0:T(256)}, f32[212]{0:T(256)S(1)}, u32[]{:S(2)}) copy-start(f32[212]{0:T(256)S(1)} %add_rsqrt_fusion) | copy-start | bytes 2548
  12.8 127.9 %copy-start.22 = (s32[212,1]{0,1:T(1,128)}, s32[212,1]{0,1:T(1,128)S(1)}, u32[]{:S(2)}) copy-start(s32[212,1]{0,1:T(1,128)S(1)} %compare_select_fusion) | copy-start | bytes 2548
  41.9 157.2 %reduce-scatter.3.cloned.1.call-start = ((), (), s32[]{:S(2)}) async-start(), calls=%async_computation.6 | async-start | bytes 5308416 | tf_op jit(solution)/shard_map/reduce_scatter | solution.py:36
  119.5 16.3 %copy-start.25 = (bf16[1,512,1024]{2,1,0:T(8,128)(2,1)S(1)}, bf16[1,512,1024]{2,1,0:T(8,128)(2,1)}, u32[]{:S(2)}) copy-start(bf16[1,512,1024]{2,1,0:T(8,128)(2,1)} %param.15) | copy-start | bytes 3145732
  134.4 1.4 copy-start.27
  140.0 68.8 %copy-start.1 = (bf16[1,212,1024]{2,1,0:T(8,128)(2,1)S(1)}, bf16[1,212,1024]{2,1,0:T(8,128)(2,1)}, u32[]{:S(2)}) copy-start(bf16[1,212,1024]{2,1,0:T(8,128)(2,1)} %param.9) | copy-start | bytes 1302532
  140.0 68.8 %copy-start.9 = (f32[1024]{0:T(1024)S(1)}, f32[1024]{0:T(1024)}, u32[]{:S(2)}) copy-start(f32[1024]{0:T(1024)} %param.12) | copy-start | bytes 12292
  140.0 69.1 %copy-start.7 = (f32[1024,32]{0,1:T(8,128)S(1)}, f32[1024,32]{0,1:T(8,128)}, u32[]{:S(2)}) copy-start(f32[1024,32]{0,1:T(8,128)} %param.13) | copy-start | bytes 393220
  140.0 69.1 %copy-start.13 = (s32[1,212,1]{1,2,0:T(1,128)S(1)}, s32[1,212,1]{1,2,0:T(1,128)}, u32[]{:S(2)}) copy-start(s32[1,212,1]{1,2,0:T(1,128)} %param.10) | copy-start | bytes 2548
  140.7 86.5 %copy-start.23 = (f32[16]{0:T(128)}, f32[16]{0:T(128)S(1)}, u32[]{:S(2)}) copy-start(f32[16]{0:T(128)S(1)} %compare_convert_fusion) | copy-start | bytes 196
  140.7 85.1 %copy-start.17 = (s32[1024]{0:T(1024)}, s32[1024]{0:T(1024)S(1)}, u32[]{:S(2)}) copy-start(s32[1024]{0:T(1024)S(1)} %pad_clamp_fusion) | copy-start | bytes 12292
  201.2 24.4 %all-to-all-start.1 = ((bf16[1,32,9,1024]{3,2,0,1:T(8,128)(2,1)}), bf16[1,32,9,1024]{3,2,0,1:T(8,128)(2,1)S(1)}, u32[]{:S(2)}, u32[]{:S(2)}) async-start(bf16[1,32,9,1024]{3,2,0,1:T(8,128)(2,1)} %bitcast.148), calls=%async_computation.2 | async-start | bytes 2097152 | tf_op jit(solution)/shard_map/all_to_all | solution.py:43
  208.7 118.1 %all-gather.9.cloned.1.call-start = ((), (), s32[]{:S(2)}) async-start(), calls=%async_computation.10 | async-start | bytes 1052672 | tf_op jit(solution)/shard_map/all_gather | solution.py:101
  209.1 0.8 copy-start.4
  209.8 16.1 %copy-start.18 = (f32[212]{0:T(256)}, f32[212]{0:T(256)S(1)}, u32[]{:S(2)}) copy-start(f32[212]{0:T(256)S(1)} %fusion.16) | copy-start | bytes 2548
  209.8 17.1 %copy-start.20 = (f32[212]{0:T(256)}, f32[212]{0:T(256)S(1)}, u32[]{:S(2)}) copy-start(f32[212]{0:T(256)S(1)} %add_divide_fusion) | copy-start | bytes 2548
  227.0 5.2 copy-start.2
  229.2 356.5 %copy-start.8 = (f32[1024]{0:T(1024)S(1)}, f32[1024]{0:T(1024)}, u32[]{:S(2)}) copy-start(f32[1024]{0:T(1024)} %broadcast_divide_fusion) | copy-start | bytes 12292
  229.2 356.5 %all-reduce.8.cloned.1.call-start = ((), (), s32[]{:S(2)}) async-start(), calls=%async_computation.12 | async-start | bytes 2097152
  230.9 357.7 %copy-start.24 = (f32[16]{0:T(128)S(1)}, f32[16]{0:T(128)}, u32[]{:S(2)}) copy-start(f32[16]{0:T(128)} %copy-done.23) | copy-start | bytes 196
  230.9 357.8 %copy-start.21 = (f32[212]{0:T(256)S(1)}, f32[212]{0:T(256)}, u32[]{:S(2)}) copy-start(f32[212]{0:T(256)} %copy-done.20) | copy-start | bytes 2548
  331.0 343.5 %all-gather.11.cloned.1.call-start = ((), (), s32[]{:S(2)}) async-start(), calls=%async_computation.11 | async-start | bytes 5308416 | tf_op jit(solution)/shard_map/all_gather | solution.py:29
  618.9 146.1 %reduce-scatter.5.cloned.1.call-start = ((), (), s32[]{:S(2)}) async-start(), calls=%async_computation.7 | async-start | bytes 5308416 | tf_op jit(solution)/shard_map/reduce_scatter | solution.py:36
  683.2 9.9 copy-start.26
  700.1 1.4 copy-start.6
  706.0 1.0 copy-start.3
  706.0 1.2 copy-start.19
  706.0 1.2 copy-start.5
  706.0 1.2 copy-start.14
  706.0 308.1 %all-reduce.6.cloned.1.call-start = ((), (), s32[]{:S(2)}) async-start(), calls=%async_computation.8 | async-start | bytes 262144 | tf_op jit(solution)/shard_map/psum | solution.py:135
  767.2 24.6 %all-to-all-start.3 = ((bf16[1,32,9,1024]{3,2,0,1:T(8,128)(2,1)}), bf16[1,32,9,1024]{3,2,0,1:T(8,128)(2,1)}, u32[]{:S(2)}, u32[]{:S(2)}) async-start(bf16[1,32,9,1024]{3,2,0,1:T(8,128)(2,1)} %bitcast.30), calls=%async_computation.5 | async-start | bytes 2097152 | tf_op jit(solution)/shard_map/all_to_all | solution.py:43
  781.8 13.4 %copy-start.10 = (f32[1024]{0:T(1024)S(1)}, f32[1024]{0:T(1024)}, u32[]{:S(2)}) copy-start(f32[1024]{0:T(1024)} %param.12) | copy-start | bytes 12292
  781.8 13.4 %copy-start.12 = (f32[212]{0:T(256)S(1)}, f32[212]{0:T(256)}, u32[]{:S(2)}) copy-start(f32[212]{0:T(256)} %copy-done.11) | copy-start | bytes 2548
  781.8 13.4 %copy-start.16 = (f32[212]{0:T(256)S(1)}, f32[212]{0:T(256)}, u32[]{:S(2)}) copy-start(f32[212]{0:T(256)} %copy-done.15) | copy-start | bytes 2548
Sparse Core Ops, SparseCore 0:
  42.0 58.8 all-gather.6
  140.1 58.9 reduce-scatter.2
  229.3 97.4 all-gather.8
  332.7 252.9 all-reduce.7
  619.1 55.3 all-gather.10
  706.1 58.9 reduce-scatter.4
  772.1 241.9 all-reduce.5
where the time goes:
time: 1020 us
  waiting for transfers between devices  736 us (72%)
  blocking collectives  125 us (12%)
  local copies, waits for them, and re-layouts  56.6 us (6%)
  matrix products  49.8 us (5%)
  between operations  19.9 us (2%)
  other arithmetic  18.6 us (2%)
  starting transfers between devices  16 us (2%)
    unnamed x8, waiting for transfers between devices  253 us
    psum x1, waiting for transfers between devices, body(): lax.psum((loss_term, router_part, gain_partial_term), ('dp', 'expert'))  141 us
    all_gather x2, waiting for transfers between devices, deliver(): whole = lax.all_gather(shaped, 'dp', axis=1, tiled=True)  114 us
    reduce_scatter x2, waiting for transfers between devices, give_back(): lax.psum_scatter(partial_value.reshape(local, n_dp, n_expert * slots, wid...  108 us
    all_gather x1, waiting for transfers between devices, body(): v_all = lax.all_gather(v, ('dp', 'expert'), axis=0, tiled=True)  94.7 us
    psum x1, blocking collectives, body(): lax.psum((loss_term, router_part, gain_partial_term), ('dp', 'expert'))  74.7 us
    all_to_all x2, blocking collectives, deliver(): lax.all_to_all(buffer.reshape(experts, 1, slots, width), 'expert', split_...  50.5 us
    all_to_all x2, waiting for transfers between devices, give_back(): lax.all_to_all(rounded, 'expert', split_axis=1, concat_axis=0, tiled=True)  25.8 us
  transfers between devices with their start and end apart: 9, of which 9 were waited for; matrix products, arithmetic and copies ran while one was open for 3% of the time, Pallas kernels for 0%

commit v1 on v0

v1 whole, which is shorter than its diff:
```python
import functools

import jax
import jax.numpy as jnp
from jax import lax
from jax.experimental import pallas as pl
from jax.experimental.pallas import tpu as pltpu
from jax.sharding import PartitionSpec as P

D = 1024
FD = 512
PATCH = 196
CAPLEN = 16
SEQ = 212
NDP = 8
NEX = 32
MAIN = NEX * 8
ROWS = NEX * 9
META = 8
HEIGHT = ROWS + META
CUT = ROWS // 2
LANES = 384
FOLD = D
EXTRA = D + 128
SEND_W = D + 256
BACK_W = D + 384
PT = 2 * NDP * NEX
LOCAL = 2 * NEX

EPS = 1e-06
LOSS_SCALE = 1024.0
BF = jnp.bfloat16
F32 = jnp.float32
I32 = jnp.int32

VM = pl.BlockSpec(memory_space=pltpu.VMEM)
SM = pl.BlockSpec(memory_space=pltpu.SMEM)


def mm(a, b, dims=((1,), (0,))):
    return lax.dot_general(a, b, (dims, ((), ())), preferred_element_type=F32)


def io(shape, axis):
    return lax.broadcasted_iota(I32, shape, axis)


def run(kernel, outs, *args, smem=0, scratch=(), name=None):
    specs = [SM] * smem + [VM] * (len(args) - smem)
    return pl.pallas_call(
        kernel,
        out_shape=outs,
        in_specs=specs,
        out_specs=jax.tree.map(lambda _: VM, outs),
        scratch_shapes=scratch,
        name=name,
        compiler_params=pltpu.CompilerParams(vmem_limit_bytes=32 * 1024 * 1024),
    )(*args)


def shape(*dims, dtype=BF):
    return jax.ShapeDtypeStruct(dims, dtype)


def spread(k):
    return (io((MAIN, NEX), 0) == io((MAIN, NEX), 1) * 8 + k).astype(BF)


def layer_norm(x):
    mean = jnp.mean(x, axis=1, keepdims=True)
    c = x - mean
    rstd = 1.0 / jnp.sqrt(jnp.mean(c * c, axis=1, keepdims=True) + EPS)
    return c * rstd, rstd


def front_kernel(length, tok, ids, gain, send, means, place):
    n = length[0]
    x = tok[...].astype(F32)
    xhat, _ = layer_norm(x)
    xn = (xhat * gain[...]).astype(BF)
    pos = io((1, SEQ), 1)
    real = pos < PATCH + n
    owner = ids[...]
    hit = (io((NEX, SEQ), 0) == owner) & real
    onehot = jnp.where(hit, 1.0, 0.0)
    before = (io((SEQ, SEQ), 0) < io((SEQ, SEQ), 1)).astype(BF)
    slot = jnp.sum(mm(onehot.astype(BF), before) * onehot, axis=0, keepdims=True).astype(I32)
    target = jnp.where(real & (slot < 8), owner * 8 + slot, -1)
    p_main = (io((MAIN, SEQ), 0) == target).astype(BF)
    p_last = jnp.where(slot == 8, onehot, 0.0).astype(BF)
    place[:MAIN] = p_main
    place[MAIN:] = p_last
    send[:, :D] = mm(p_main, xn).astype(BF)
    last = mm(p_last, xn).astype(BF)
    fold = mm(spread(0), last[:, :128])
    for k in range(1, 8):
        fold = fold + mm(spread(k), last[:, 128 * k : 128 * (k + 1)])
    send[:, FOLD:EXTRA] = fold.astype(BF)
    images = jnp.sum(jnp.where(pos < PATCH, onehot, 0.0), axis=1, keepdims=True)
    lane = io((NEX, 128), 1)
    info = jnp.where(lane == 0, images, jnp.where(lane == 1, n.astype(F32), 0.0)).astype(BF)
    send[:, EXTRA:] = mm(spread(0), info).astype(BF)
    at = io((SEQ, 1), 0)
    w_img = jnp.where(at < PATCH, 1.0 / PATCH, 0.0)
    w_cap = jnp.where((at >= PATCH) & (at < PATCH + n), 1.0 / n.astype(F32), 0.0)
    means[0:1] = jnp.sum(x * w_img, axis=0, keepdims=True)
    means[1:2] = jnp.sum(x * w_cap, axis=0, keepdims=True)


def unpack_kernel(got, block):
    block[:MAIN] = got[:, :D]
    info = mm(spread(0), got[:, EXTRA:SEND_W], ((0,), (0,)))
    fold = got[:, FOLD:EXTRA]
    for k in range(8):
        block[MAIN:ROWS, 128 * k : 128 * (k + 1)] = mm(spread(k), fold, ((0,), (0,))).astype(BF)
    r = io((1, LANES), 1)
    ex = jnp.where(r < MAIN, r // 8, r - MAIN)
    slot = jnp.where(r < MAIN, r % 8, 8).astype(F32)
    match = io((NEX, LANES), 0) == ex
    images = jnp.sum(jnp.where(match, info[:, 0:1], 0.0), axis=0, keepdims=True)
    lens = jnp.sum(jnp.where(match, info[:, 1:2], 0.0), axis=0, keepdims=True)
    is_img = slot < images
    pt = jnp.where(r < ROWS, 2 * ex + jnp.where(is_img, 0, 1), LOCAL).astype(F32)
    div = jnp.where(r < ROWS, jnp.where(is_img, float(PATCH), lens), 1.0)
    sub = io((META, LANES), 0)
    block[ROWS:, :LANES] = jnp.where(sub == 0, pt, jnp.where(sub == 1, div, 0.0)).astype(BF)
    block[ROWS:, LANES:] = jnp.zeros((META, D - LANES), BF)


CHUNK = 32


def forward_kernel(x, wu, router, act, slope, cols, pooled, pre, mixed):
    pre[...] = mm(x[:ROWS], wu[...])
    meta = x[ROWS:, :LANES].astype(F32)
    pt_row = meta[0:1]
    div_row = meta[1:2]

    def step(c, _):
        at = pl.ds(pl.multiple_of(c * CHUNK, CHUNK), CHUNK)
        xc = x[at, :].astype(F32)
        gate = jax.nn.sigmoid(jnp.sum(xc * router[...], axis=1, keepdims=True))
        diag = io((CHUNK, LANES), 1) == io((CHUNK, LANES), 0) + c * CHUNK
        div = jnp.sum(jnp.where(diag, div_row, 0.0), axis=1, keepdims=True)
        pt = jnp.sum(jnp.where(diag, pt_row, 0.0), axis=1, keepdims=True)
        scaled = gate / div
        p = pre[at, :]
        phi = 0.5 * (1.0 + lax.erf(p * 0.7071067811865476))
        a = (p * phi).astype(BF)
        act[at, :] = a
        slope[at, :] = (phi + p * jnp.exp(-0.5 * p * p) * 0.3989422804014327).astype(BF)
        mixed[at, :] = (scaled * a.astype(F32)).astype(BF)
        lane = io((CHUNK, 128), 1)
        cols[at, :] = jnp.where(lane == 0, scaled, jnp.where(lane == 1, 1.0 - gate, jnp.where(lane == 2, pt, 0.0)))
        return 0

    lax.fori_loop(0, ROWS // CHUNK, step, 0)
    sel = (io((LOCAL, ROWS), 0).astype(F32) == pt_row[:, :ROWS]).astype(BF)
    pooled[...] = mm(sel, mixed[...]).astype(BF)


def forward_block(x, wu, router):
    return run(
        forward_kernel,
        (shape(ROWS, FD), shape(ROWS, FD), shape(ROWS, 128, dtype=F32), shape(LOCAL, FD)),
        x,
        wu,
        router,
        scratch=[pltpu.VMEM((ROWS, FD), F32), pltpu.VMEM((ROWS, FD), BF)],
        name="expert_forward",
    )


def part_kernel(offsets, me, *refs):
    wd, part, pooled = refs[NDP:]
    total = None
    g = io((PT, LOCAL), 0)
    p = io((PT, LOCAL), 1)
    for ref, off in zip(refs[:NDP], offsets):
        src = (me[0] + off) % NDP
        perm = (g == (p // 2) * (2 * NDP) + src * 2 + p % 2).astype(BF)
        term = mm(perm, ref[...])
        total = term if total is None else total + term
    pooled[...] = total.astype(BF)
    part[...] = mm(pooled[...], wd[...]).astype(BF)


def column_kernel(me, got, means, out):
    s = jnp.sum(got[...].astype(F32), axis=0)
    row = io((2 * NDP, 1), 0)
    own = row // 2 == me[0]
    s = s + jnp.where(own & (row % 2 == 0), means[0:1], 0.0) + jnp.where(own & (row % 2 == 1), means[1:2], 0.0)
    out[...] = jnp.broadcast_to(s.astype(BF)[None], (NDP, 2 * NDP, D))


def share_kernel(got, out):
    s = jnp.sum(got[...].astype(F32), axis=0)
    out[...] = jnp.broadcast_to(s.astype(BF)[None], (NEX, 2 * NDP, D))


def loss_kernel(me, scale, bias, emb, wd, loss, d_emb, dy, q, dots, inv_col, high, low, grads):
    e = emb[...]
    dots[...] = mm(e, e, ((1,), (1,)))
    to_unit = scale[0] / D
    step_rows = 64
    steps = PT // step_rows

    def norms(c, row_sum):
        at = pl.ds(pl.multiple_of(c * step_rows, step_rows), step_rows)
        diag = io((step_rows, PT), 1) == io((step_rows, PT), 0) + c * step_rows
        on = jnp.where(diag, dots[at, :], 0.0)
        inv = 1.0 / jnp.sqrt(jnp.sum(on, axis=1, keepdims=True) / D + EPS)
        inv_col[at, :] = jnp.broadcast_to(inv, (step_rows, 128))
        return row_sum + jnp.sum(on, axis=0, keepdims=True)

    squares = lax.fori_loop(0, steps, norms, jnp.zeros((1, PT), F32))
    inv_row = 1.0 / jnp.sqrt(squares / D + EPS)

    def terms(c, total):
        at = pl.ds(pl.multiple_of(c * step_rows, step_rows), step_rows)
        i = io((step_rows, PT), 0) + c * step_rows
        j = io((step_rows, PT), 1)
        same = i // 2 == j // 2
        sign = jnp.where(same, 1.0, -1.0)
        cross = i % 2 != j % 2
        z = sign * (dots[at, :] * to_unit * inv_col[at, 0:1] * inv_row + bias[0])
        t = jnp.exp(-jnp.abs(z))
        soft = jnp.maximum(-z, 0.0) + jnp.log1p(t)
        sig = jnp.where(z >= 0.0, t, 1.0) / (1.0 + t)
        coef = jnp.where(cross, (-LOSS_SCALE / (PT // 2)) * sign * sig, 0.0) * inv_row * to_unit
        hi = coef.astype(BF)
        high[at, :] = hi
        low[at, :] = (coef - hi.astype(F32)).astype(BF)
        return total + jnp.sum(jnp.where(cross & (i % 2 == 0), soft, 0.0), axis=0, keepdims=True)

    total = lax.fori_loop(0, steps, terms, jnp.zeros((1, PT), F32))
    loss[...] = jnp.sum(total, axis=1, keepdims=True) / (PT // 2)
    grads[...] = mm(high[...], e) + mm(low[...], e)

    def project(c, _):
        at = pl.ds(pl.multiple_of(c * step_rows, step_rows), step_rows)
        inv = inv_col[at, 0:1]
        unit = emb[at, :].astype(F32) * inv
        dw = grads[at, :]
        res = (dw - unit * (jnp.sum(dw * unit, axis=1, keepdims=True) / D)) * inv
        grads[at, :] = res
        d_emb[at, :] = res.astype(BF)
        return 0

    lax.fori_loop(0, steps, project, 0)
    first = (me[1] * NDP + me[0]) * 2
    base = pl.multiple_of((first // 8) * 8, 8)
    near = grads[pl.ds(base, 8), :]
    row = io((8, 1), 0)
    dy[0:1] = jnp.sum(jnp.where(row == first % 8, near, 0.0), axis=0, keepdims=True)
    dy[1:2] = jnp.sum(jnp.where(row == first % 8 + 1, near, 0.0), axis=0, keepdims=True)
    raw = mm(d_emb[...], wd[...], ((1,), (1,))).astype(BF)
    i = io((PT, PT), 0)
    at = (i % LOCAL) // 2 * (2 * NDP) + (i // LOCAL) * 2 + i % 2
    perm = (io((PT, PT), 1) == at).astype(BF)
    q[...] = mm(perm, raw).astype(BF)


def slope_kernel(off, me, q, act, slope, cols, dpre, dgl):
    src = (me[0] + off) % NDP
    qb = q[pl.ds(pl.multiple_of(src * LOCAL, LOCAL), LOCAL), :]

    def step(c, _):
        at = pl.ds(pl.multiple_of(c * CHUNK, CHUNK), CHUNK)
        col = cols[at, :]
        pick = (io((CHUNK, LOCAL), 1).astype(F32) == col[:, 2:3]).astype(BF)
        dact = mm(pick, qb) * col[:, 0:1]
        dpre[at, :] = (dact * slope[at, :].astype(F32)).astype(BF)
        dots = jnp.sum(dact * act[at, :].astype(F32), axis=1, keepdims=True) * col[:, 1:2]
        dgl[at, :] = jnp.broadcast_to(dots, (CHUNK, 128))
        return 0

    lax.fori_loop(0, ROWS // CHUNK, step, 0)


def slope_block(off, me, q, saved):
    _, act, slope, cols, _ = saved
    return run(
        functools.partial(slope_kernel, off),
        (shape(ROWS, FD), shape(ROWS, 128, dtype=F32)),
        me,
        q,
        act,
        slope,
        cols,
        smem=1,
        name="expert_slope",
    )


def back_value(dpre, dgl, wu, router):
    return mm(dpre[...], wu[...], ((1,), (1,))) + dgl[:, 0:1] * router[...]


def back_first_kernel(dpre, dgl, wu, router, top, low):
    v = back_value(dpre, dgl, wu, router)
    top[...] = v[:CUT].astype(BF)
    low[...] = v[CUT:].astype(BF)


def back_half_kernel(upper, dpre, dgl, wu, router, part, out):
    v = back_value(dpre, dgl, wu, router)
    if upper:
        out[:CUT] = (v[:CUT] + part[...].astype(F32)).astype(BF)
        out[CUT:] = v[CUT:].astype(BF)
    else:
        out[:CUT] = v[:CUT].astype(BF)
        out[CUT:] = (v[CUT:] + part[...].astype(F32)).astype(BF)


def back_kernel(dpre, dgl, wu, router, part, out):
    v = back_value(dpre, dgl, wu, router)
    out[...] = (v + part[...].astype(F32)).astype(BF)


def back_last_kernel(own, r, l, small, send):
    v = (own[...] + r[...].astype(F32) + l[...].astype(F32)).astype(BF)
    send[:, :D] = v[:MAIN]
    last = v[MAIN:]
    fold = mm(spread(0), last[:, :128])
    for k in range(1, 8):
        fold = fold + mm(spread(k), last[:, 128 * k : 128 * (k + 1)])
    send[:, FOLD:EXTRA] = fold.astype(BF)
    total = jnp.sum(small[...], axis=0)
    sub = io((MAIN, 128), 0) % 8
    for n in range(2):
        value = jnp.zeros((MAIN, 128), F32)
        for k in range(8):
            value = jnp.where(sub == k, total[n : n + 1, 128 * k : 128 * (k + 1)], value)
        send[:, EXTRA + 128 * n : EXTRA + 128 * (n + 1)] = value.astype(BF)


def back_own_kernel(dpre, dgl, wu, router, out):
    out[...] = back_value(dpre, dgl, wu, router)


def weight_kernel(*refs):
    xs, dpres, dgls = refs[:NDP], refs[NDP : 2 * NDP], refs[2 * NDP : 3 * NDP]
    wu, router, grad_up, small, cat = refs[3 * NDP :]
    for n, (x, dpre) in enumerate(zip(xs, dpres)):
        term = mm(x[:ROWS], dpre[...], ((0,), (0,)))
        if n == 0:
            grad_up[...] = term
        else:
            grad_up[...] += term
    g_router = None
    for x, dgl in zip(xs, dgls):
        term = jnp.sum(x[:ROWS].astype(F32) * dgl[:, 0:1], axis=0, keepdims=True)
        g_router = term if g_router is None else g_router + term
    cat[...] = wu[...].astype(F32) * grad_up[...]
    rows = lax.dot_general(
        jnp.ones((8, FD), F32), cat[...], (((1,), (1,)), ((), ())), precision=lax.Precision.HIGHEST, preferred_element_type=F32
    )
    both = jnp.concatenate([g_router, rows[0:1] + g_router * router[...]], axis=0)
    small[...] = jnp.broadcast_to(both[None], (NDP, 2, D))


def down_kernel(pooled, d_emb, out):
    out[...] = mm(pooled[...], d_emb[...], ((0,), (0,)))


def final_kernel(length, tok, gain, place, got, dy, grad_tokens, grad_router, gain_grad):
    n = length[0]
    xhat, rstd = layer_norm(tok[...].astype(F32))
    fold = got[:, FOLD:EXTRA]
    ones = [mm(spread(k), fold, ((0,), (0,))).astype(BF) for k in range(8)]
    last = jnp.concatenate(ones, axis=1)
    dxn = mm(place[:MAIN], got[:, :D], ((0,), (0,))) + mm(place[MAIN:], last, ((0,), (0,)))
    at = io((SEQ, 1), 0)
    w_img = jnp.where(at < PATCH, 1.0 / PATCH, 0.0)
    w_cap = jnp.where((at >= PATCH) & (at < PATCH + n), 1.0 / n.astype(F32), 0.0)
    g = dxn * gain[...]
    inner = jnp.sum(g * xhat, axis=1, keepdims=True) / D
    dx = (g - jnp.mean(g, axis=1, keepdims=True) - xhat * inner) * rstd
    grad_tokens[...] = (dx + w_img * dy[0:1] + w_cap * dy[1:2]).astype(BF)
    for k in range(8):
        piece = mm(spread(k), got[:, EXTRA:], ((0,), (0,)))
        grad_router[:, 128 * k : 128 * (k + 1)] = piece[:, :128]
        at_k = slice(128 * k, 128 * (k + 1))
        gain_grad[:, at_k] = jnp.sum(piece[:, 128:], axis=0, keepdims=True) / gain[:, at_k]


def exchange(value, axis):
    return lax.all_to_all(value, axis, split_axis=0, concat_axis=0, tiled=True)


def body(tokens, expert_ids, caption_lengths, gain, router, w_up, w_down, logit_scale, logit_bias):
    me_dp = lax.axis_index("dp").astype(I32)
    me_ex = lax.axis_index("expert").astype(I32)
    me = jnp.stack([me_dp, me_ex])
    wu = w_up[0]
    wd = w_down[0]
    tok = tokens[0]
    gain_row = gain.reshape(1, D)
    send, means, place = run(
        front_kernel,
        (shape(MAIN, SEND_W), shape(2, D, dtype=F32), shape(ROWS, SEQ)),
        caption_lengths,
        tok,
        expert_ids.reshape(1, SEQ),
        gain_row,
        smem=1,
        name="front",
    )
    got = exchange(send.reshape(NEX, 8, SEND_W), "expert").reshape(MAIN, SEND_W)
    own = run(unpack_kernel, shape(HEIGHT, D), got, name="unpack")

    right = [(i, (i + 1) % NDP) for i in range(NDP)]
    left = [(i, (i - 1) % NDP) for i in range(NDP)]
    half = NDP // 2
    router_row = jnp.sum(jnp.where(jnp.arange(NEX, dtype=I32)[None, :] == me_ex, router, 0.0), axis=1).reshape(1, D)
    r, l = own, own
    xs = {0: own}
    for k in range(1, half):
        r = lax.ppermute(r, "dp", right)
        l = lax.ppermute(l, "dp", left)
        xs[-k], xs[k] = r, l
    r = lax.ppermute(r[:CUT], "dp", right)
    l = lax.ppermute(l[CUT:], "dp", left)
    xs[half] = jnp.concatenate([r, l], axis=0)
    offsets = list(xs)
    saved = {off: (x,) + tuple(forward_block(x, wu, router_row)) for off, x in xs.items()}
    part, pooled = run(
        functools.partial(part_kernel, offsets),
        (shape(PT, D), shape(PT, FD)),
        me,
        *[saved[off][4] for off in offsets],
        wd,
        smem=1,
        name="pooled_down",
    )
    part = exchange(part.reshape(NEX, 2 * NDP, D), "expert")
    column = run(column_kernel, shape(NDP, 2 * NDP, D), me, part, means, smem=1, name="column")
    column = exchange(column, "dp")
    shared = run(share_kernel, shape(NEX, 2 * NDP, D), column, name="share")
    emb = exchange(shared, "expert").reshape(PT, D)
    loss, d_emb, dy, q = run(
        loss_kernel,
        (shape(1, 1, dtype=F32), shape(PT, D), shape(2, D, dtype=F32), shape(PT, FD)),
        me,
        logit_scale,
        logit_bias,
        emb,
        wd,
        smem=3,
        scratch=[
            pltpu.VMEM((PT, PT), F32),
            pltpu.VMEM((PT, 128), F32),
            pltpu.VMEM((PT, PT), BF),
            pltpu.VMEM((PT, PT), BF),
            pltpu.VMEM((PT, D), F32),
        ],
        name="pair_loss",
    )

    slopes = {half: slope_block(half, me, q, saved[half])}
    r, l = run(back_first_kernel, (shape(CUT, D), shape(CUT, D)), *slopes[half], wu, router_row, name="back_first")
    for off in (half - 1, 1 - half, 2, -2, 1, -1, 0):
        slopes[off] = slope_block(off, me, q, saved[off])
    for k in range(half - 1, -1, -1):
        r = lax.ppermute(r, "dp", right)
        l = lax.ppermute(l, "dp", left)
        if k == half - 1:
            r = run(functools.partial(back_half_kernel, True), shape(ROWS, D), *slopes[k], wu, router_row, r, name="back_half")
            l = run(functools.partial(back_half_kernel, False), shape(ROWS, D), *slopes[-k], wu, router_row, l, name="back_half")
        elif k > 0:
            r = run(back_kernel, shape(ROWS, D), *slopes[k], wu, router_row, r, name="back")
            l = run(back_kernel, shape(ROWS, D), *slopes[-k], wu, router_row, l, name="back")
    grad_up, small = run(
        weight_kernel,
        (shape(D, FD, dtype=F32), shape(NDP, 2, D, dtype=F32)),
        *[xs[off] for off in offsets],
        *[slopes[off][0] for off in offsets],
        *[slopes[off][1] for off in offsets],
        wu,
        router_row,
        scratch=[pltpu.VMEM((D, FD), F32)],
        name="weight_grads",
    )
    grad_down = run(down_kernel, shape(FD, D, dtype=F32), pooled, d_emb, name="down_grad")
    small = exchange(small, "dp")
    own_back = run(back_own_kernel, shape(ROWS, D, dtype=F32), *slopes[0], wu, router_row, name="back_own")
    send = run(back_last_kernel, shape(MAIN, BACK_W), own_back, r, l, small, name="back_last")
    got = exchange(send.reshape(NEX, 8, BACK_W), "expert").reshape(MAIN, BACK_W)
    grad_tokens, grad_router, gain_grad = run(
        final_kernel,
        (shape(SEQ, D), shape(NEX, D, dtype=F32), shape(1, D, dtype=F32)),
        caption_lengths,
        tok,
        gain_row,
        place,
        got,
        dy,
        smem=1,
        name="final",
    )
    return (loss.reshape(1), grad_tokens[None], grad_up[None], grad_down[None], grad_router.T, gain_grad.reshape(D))


def solution(mesh):
    return jax.shard_map(
        body,
        mesh=mesh,
        in_specs=(
            P(("dp", "expert"), None, None),
            P(("dp", "expert"), None, None),
            P(("dp", "expert")),
            P(),
            P(),
            P("expert", None, "dp"),
            P("expert", "dp", None),
            P(),
            P(),
        ),
        out_specs=(
            P(),
            P(("dp", "expert"), None, None),
            P("expert", None, "dp"),
            P("expert", "dp", None),
            P(),
            P(),
        ),
        check_vma=False,
    )
```

time: 1020 us -> 286 us (0.28)
  waiting for transfers between devices: 736 us -> 78.1 us
  Pallas kernels: 0 us -> 82.2 us
  blocking collectives: 125 us -> 60.9 us
  matrix products: 49.8 us -> 0 us
  local copies, waits for them, and re-layouts: 56.6 us -> 19.9 us
  starting transfers between devices: 16 us -> 41.1 us
  other arithmetic: 18.6 us -> 0.17 us
  between operations: 19.9 us -> 3.27 us
    unnamed x8 -> x0, waiting for transfers between devices: 253 us -> none
    all_gather x3 -> x0, waiting for transfers between devices: 209 us -> none  [the longest x2 114 us: deliver(): whole = lax.all_gather(shaped, 'dp', axis=1, tiled=True)]
    psum x1 -> x0, waiting for transfers between devices: 141 us -> none  [body(): lax.psum((loss_term, router_part, gain_partial_term), ('dp', 'expert'))]
    reduce_scatter x2 -> x0, waiting for transfers between devices: 108 us -> none  [give_back(): lax.psum_scatter(partial_value.reshape(local, n_dp, n_expert * slots, wid...]
    pallas_call x0 -> x34, Pallas kernels: none -> 82.2 us  [run(): pl.pallas_call(kernel, out_shape=outs, in_specs=specs, out_specs=jax.tree...]
    psum x1 -> x0, blocking collectives: 74.7 us -> none  [body(): lax.psum((loss_term, router_part, gain_partial_term), ('dp', 'expert'))]
    dot_general x11 -> x0, matrix products: 49.8 us -> none  [the longest x1 14.9 us: body(): jnp.einsum('erd,edf->erf', gathered, w_up, preferred_element_type=jnp.flo...]
    ppermute x0 -> x16, waiting for transfers between devices: none -> 45.2 us  [the longest x7 38.2 us: body(): r = lax.ppermute(r, 'dp', right)]
  transfers between devices with their start and end apart: 9 -> 19, of which waited for: 9 -> 8; matrix products, arithmetic and copies ran while one was open for 3% -> 0% of each run, Pallas kernels for 0% -> 20%
where the time goes in v1:
time: 286 us
  Pallas kernels  82.2 us (29%)
  waiting for transfers between devices  78.1 us (27%)
  blocking collectives  60.9 us (21%)
  starting transfers between devices  41.1 us (14%)
  local copies, waits for them, and re-layouts  19.9 us (7%)
  between operations  3.27 us (1%)
    pallas_call x34, Pallas kernels, run(): pl.pallas_call(kernel, out_shape=outs, in_specs=specs, out_specs=jax.tree...  82.2 us
    all_to_all x3, blocking collectives, exchange(): return lax.all_to_all(value, axis, split_axis=0, concat_axis=0, tiled=True)  60.9 us
    ppermute x7, waiting for transfers between devices, body(): r = lax.ppermute(r, 'dp', right)  38.2 us
    all_to_all x3, waiting for transfers between devices, exchange(): return lax.all_to_all(value, axis, split_axis=0, concat_axis=0, tiled=True)  32.9 us
    unnamed x141, local copies, waits for them, and re-layouts  19.8 us
    ppermute x7, starting transfers between devices, body(): l = lax.ppermute(l, 'dp', left)  17.7 us
    all_to_all x3, starting transfers between devices, exchange(): return lax.all_to_all(value, axis, split_axis=0, concat_axis=0, tiled=True)  16.6 us
    ppermute x7, waiting for transfers between devices, body(): l = lax.ppermute(l, 'dp', left)  7.02 us
  transfers between devices with their start and end apart: 19, of which 8 were waited for; matrix products, arithmetic and copies ran while one was open for 0% of the time, Pallas kernels for 20%

profile of v1, /device:TPU:1, one launch (start us, length us, event | category | flops | bytes accessed | tf_op | source)
XLA Modules:
  0.0 285.7 jit_solution(6641203472358920588)
XLA Ops:
  4.8 21.3 %all_to_all.30 = bf16[32,8,1280]{2,1,0:T(8,128)(2,1)S(1)} all-to-all(bf16[32,8,1280]{2,1,0:T(8,128)(2,1)S(1)} %bitcast.61), channel_id=1, replica_groups=mesh['dp'=8,'expert'=32] {'expert'}, dimensions={0} | all-to-all | bytes 1310720 | tf_op jit(solution)/shard_map/all_to_all | solution.py:389
  26.4 1.7 collective-permute-start
  28.1 4.0 %collective-permute-start.1 = (bf16[296,1024]{1,0:T(8,128)(2,1)S(1)}, bf16[296,1024]{1,0:T(8,128)(2,1)S(1)}, u32[]{:S(2)}, u32[]{:S(2)}) collective-permute-start(bf16[296,1024]{1,0:T(8,128)(2,1)S(1)} %unpack.1.x.refs_0_), channel_id=1, source_target_pairs={{0,224},{32,0},{64,32},{96,64},{128,96},{160,128},{192,160},{224,1... | collective-permute-start | bytes 1818632 | tf_op jit(solution)/shard_map/ppermute | solution.py:421
  32.2 14.1 %collective-permute-done.x.refs_1_ = bf16[296,1024]{1,0:T(8,128)(2,1)S(1)} collective-permute-done((bf16[296,1024]{1,0:T(8,128)(2,1)S(1)}, bf16[296,1024]{1,0:T(8,128)(2,1)S(1)}, u32[]{:S(2)}, u32[]{:S(2)}) %collective-permute-start) | collective-permute-done | bytes 606240 | tf_op jit(solution)/shard_map/ppermute | solution.py:420
  47.1 2.7 collective-permute-start.3
  50.6 11.8 %collective-permute-done.2.x.refs_3_ = bf16[296,1024]{1,0:T(8,128)(2,1)} collective-permute-done((bf16[296,1024]{1,0:T(8,128)(2,1)S(1)}, bf16[296,1024]{1,0:T(8,128)(2,1)}, u32[]{:S(2)}, u32[]{:S(2)}) %collective-permute-start.2) | collective-permute-done | bytes 606240 | tf_op jit(solution)/shard_map/ppermute | solution.py:420
  62.5 3.2 %collective-permute-start.5 = (bf16[296,1024]{1,0:T(8,128)(2,1)}, bf16[296,1024]{1,0:T(8,128)(2,1)S(1)}, u32[]{:S(2)}, u32[]{:S(2)}) collective-permute-start(bf16[296,1024]{1,0:T(8,128)(2,1)} %collective-permute-done.3.x.refs_4_), channel_id=1, source_target_pairs={{0,224},{32,0},{64,32},{96,64},{128,96},{160,128},{192,160},{224,1... | collective-permute-start | bytes 1818632 | tf_op jit(solution)/shard_map/ppermute | solution.py:421
  65.7 12.2 %collective-permute-done.4.x.refs_5_ = bf16[296,1024]{1,0:T(8,128)(2,1)S(1)} collective-permute-done((bf16[296,1024]{1,0:T(8,128)(2,1)}, bf16[296,1024]{1,0:T(8,128)(2,1)S(1)}, u32[]{:S(2)}, u32[]{:S(2)}) %collective-permute-start.4) | collective-permute-done | bytes 606240 | tf_op jit(solution)/shard_map/ppermute | solution.py:420
  78.0 3.0 %collective-permute-start.7 = (bf16[152,1024]{1,0:T(8,128)(2,1)S(1)}, bf16[152,1024]{1,0:T(8,128)(2,1)S(1)}, u32[]{:S(2)}, u32[]{:S(2)}) collective-permute-start(bf16[152,1024]{1,0:T(8,128)(2,1)S(1)} %slice.9), channel_id=1, source_target_pairs={{0,224},{32,0},{64,32},{96,64},{128,96},{160,128},{192,160},{224,1... | collective-permute-start | bytes 933896 | tf_op jit(solution)/shard_map/ppermute | solution.py:424
  81.2 1.6 expert_forward.8
  82.9 1.7 expert_forward.9
  86.6 1.6 expert_forward.10
  88.3 2.9 %expert_forward.11 = (bf16[288,512]{1,0:T(8,128)(2,1)S(1)}, bf16[288,512]{1,0:T(8,128)(2,1)S(1)}, f32[288,128]{1,0:T(8,128)S(1)}, bf16[64,512]{1,0:T(8,128)(2,1)S(1)}) custom-call(bf16[296,1024]{1,0:T(8,128)(2,1)} %collective-permute-done.2.x.refs_3_, bf16[1024,512]{1,0:T(8,128)(2,1)S(1)} %bitcast.23, f32[1,1024]{1,0:T(1,128)S(1)} %bitcast.46), custom_call_target="tpu_custom_call" | custom-call | tf_op jit(solution)/shard_map/expert_forward/pallas_call | solution.py:50
  93.4 2.7 expert_forward.12
  98.2 1.6 expert_forward.13
  102.0 1.6 expert_forward.14
  105.1 1.6 expert_forward.15
  109.6 2.3 pooled_down.1
  112.8 22.5 %all_to_all.31.got = bf16[32,16,1024]{2,1,0:T(8,128)(2,1)S(1)} all-to-all(bf16[32,16,1024]{2,1,0:T(8,128)(2,1)S(1)} %bitcast.60), channel_id=1, replica_groups=mesh['dp'=8,'expert'=32] {'expert'}, dimensions={0} | all-to-all | bytes 2097152 | tf_op jit(solution)/shard_map/all_to_all | solution.py:389
  135.9 17.1 %all_to_all.32.got = bf16[8,16,1024]{2,1,0:T(8,128)(2,1)S(1)} all-to-all(bf16[8,16,1024]{2,1,0:T(8,128)(2,1)S(1)} %column.1), channel_id=1, replica_groups=mesh['dp'=8,'expert'=32] {'dp'}, dimensions={0} | all-to-all | bytes 524288 | tf_op jit(solution)/shard_map/all_to_all | solution.py:389
  153.0 1.1 share.1
  154.1 4.8 %all-to-all-start.3 = ((bf16[32,16,1024]{2,1,0:T(8,128)(2,1)}), bf16[32,16,1024]{2,1,0:T(8,128)(2,1)}, u32[]{:S(2)}, u32[]{:S(2)}) async-start(bf16[32,16,1024]{2,1,0:T(8,128)(2,1)} %share.1), calls=%async_computation.3 | async-start | bytes 2097152 | tf_op jit(solution)/shard_map/all_to_all | solution.py:389
  160.2 15.8 %all-to-all-done.3 = bf16[32,16,1024]{2,1,0:T(8,128)(2,1)} async-done(((bf16[32,16,1024]{2,1,0:T(8,128)(2,1)}), bf16[32,16,1024]{2,1,0:T(8,128)(2,1)}, u32[]{:S(2)}, u32[]{:S(2)}) %all-to-all-start.3) | async-done | bytes 1048608 | tf_op jit(solution)/shard_map/all_to_all | solution.py:389
  176.0 9.0 %pair_loss.1 = (f32[1,1]{1,0:T(1,128)}, bf16[512,1024]{1,0:T(8,128)(2,1)S(1)}, f32[2,1024]{1,0:T(2,128)S(1)}, bf16[512,512]{1,0:T(8,128)(2,1)S(1)}) custom-call(s32[2]{0:T(128)S(1)} %pad_add_fusion.me, f32[1]{0:T(128)S(6)} %copy.17.scale, f32[1]{0:T(128)S(6)} %copy.18.bias, bf16[512,1024]{1,0:T(8,128)(2,1)} %bitcast.11.emb, bf16[512,1024]{1,0:T(8,128)(2,1)S(1)} %bitcast.38), custom_call_target="tpu_custom_call" | custom-call | tf_op jit(solution)/shard_map/pair_loss/pallas_call | solution.py:50
  186.0 3.9 %expert_slope.12 = (bf16[288,512]{1,0:T(8,128)(2,1)S(1)}, f32[288,128]{1,0:T(8,128)S(1)}) custom-call(s32[2]{0:T(128)S(1)} %pad_add_fusion.me, bf16[512,512]{1,0:T(8,128)(2,1)S(1)} %get-tuple-element.83.q, bf16[288,512]{1,0:T(8,128)(2,1)S(1)} %copy-done.47, bf16[288,512]{1,0:T(8,128)(2,1)S(1)} %copy-done.49, f32[288,128]{1,0:T(8,128)S(1)} %copy-done.65), custom_call_target="tpu_custom_call" | custom-call | tf_op jit(solution)/shard_map/expert_slope/pallas_call | solution.py:50
  190.5 1.5 collective-permute-start.8
  192.0 3.9 %expert_slope.15 = (bf16[288,512]{1,0:T(8,128)(2,1)S(1)}, f32[288,128]{1,0:T(8,128)S(1)}) custom-call(s32[2]{0:T(128)S(1)} %pad_add_fusion.me, bf16[512,512]{1,0:T(8,128)(2,1)S(1)} %get-tuple-element.83.q, bf16[288,512]{1,0:T(8,128)(2,1)S(1)} %copy-done.43, bf16[288,512]{1,0:T(8,128)(2,1)S(1)} %copy-done.45, f32[288,128]{1,0:T(8,128)S(1)} %copy-done.63), custom_call_target="tpu_custom_call" | custom-call | tf_op jit(solution)/shard_map/expert_slope/pallas_call | solution.py:50
  195.9 3.9 %expert_slope.11 = (bf16[288,512]{1,0:T(8,128)(2,1)S(1)}, f32[288,128]{1,0:T(8,128)S(1)}) custom-call(s32[2]{0:T(128)S(1)} %pad_add_fusion.me, bf16[512,512]{1,0:T(8,128)(2,1)S(1)} %get-tuple-element.83.q, bf16[288,512]{1,0:T(8,128)(2,1)S(1)} %copy-done.39, bf16[288,512]{1,0:T(8,128)(2,1)S(1)} %copy-done.41, f32[288,128]{1,0:T(8,128)S(1)} %copy-done.61), custom_call_target="tpu_custom_call" | custom-call | tf_op jit(solution)/shard_map/expert_slope/pallas_call | solution.py:50
  200.3 1.4 collective-permute-start.13
  202.7 3.9 %expert_slope.14 = (bf16[288,512]{1,0:T(8,128)(2,1)S(1)}, f32[288,128]{1,0:T(8,128)S(1)}) custom-call(s32[2]{0:T(128)S(1)} %pad_add_fusion.me, bf16[512,512]{1,0:T(8,128)(2,1)S(1)} %get-tuple-element.83.q, bf16[288,512]{1,0:T(8,128)(2,1)S(1)} %copy-done.35, bf16[288,512]{1,0:T(8,128)(2,1)S(1)} %copy-done.37, f32[288,128]{1,0:T(8,128)S(1)} %copy-done.59), custom_call_target="tpu_custom_call" | custom-call | tf_op jit(solution)/shard_map/expert_slope/pallas_call | solution.py:50
  206.6 3.9 %expert_slope.10 = (bf16[288,512]{1,0:T(8,128)(2,1)S(1)}, f32[288,128]{1,0:T(8,128)S(1)}) custom-call(s32[2]{0:T(128)S(1)} %pad_add_fusion.me, bf16[512,512]{1,0:T(8,128)(2,1)S(1)} %get-tuple-element.83.q, bf16[288,512]{1,0:T(8,128)(2,1)S(1)} %copy-done.31, bf16[288,512]{1,0:T(8,128)(2,1)S(1)} %copy-done.33, f32[288,128]{1,0:T(8,128)S(1)} %copy-done.57), custom_call_target="tpu_custom_call" | custom-call | tf_op jit(solution)/shard_map/expert_slope/pallas_call | solution.py:50
  210.5 4.1 %collective-permute-done.13.part = bf16[288,1024]{1,0:T(8,128)(2,1)S(1)} collective-permute-done((bf16[288,1024]{1,0:T(8,128)(2,1)S(1)}, bf16[288,1024]{1,0:T(8,128)(2,1)S(1)}, u32[]{:S(2)}, u32[]{:S(2)}) %collective-permute-start.13) | collective-permute-done | bytes 589856 | tf_op jit(solution)/shard_map/ppermute | solution.py:467
  215.1 2.9 %collective-permute-start.14 = (bf16[288,1024]{1,0:T(8,128)(2,1)S(1)}, bf16[288,1024]{1,0:T(8,128)(2,1)S(1)}, u32[]{:S(2)}, u32[]{:S(2)}) collective-permute-start(bf16[288,1024]{1,0:T(8,128)(2,1)S(1)} %back.6), channel_id=1, source_target_pairs={{0,224},{32,0},{64,32},{96,64},{128,96},{160,128},{192,160},{224,1... | collective-permute-start | bytes 1769480 | tf_op jit(solution)/shard_map/ppermute | solution.py:467
  218.7 3.9 %expert_slope.13 = (bf16[288,512]{1,0:T(8,128)(2,1)S(1)}, f32[288,128]{1,0:T(8,128)S(1)}) custom-call(s32[2]{0:T(128)S(1)} %pad_add_fusion.me, bf16[512,512]{1,0:T(8,128)(2,1)S(1)} %get-tuple-element.83.q, bf16[288,512]{1,0:T(8,128)(2,1)S(1)} %copy-done.27, bf16[288,512]{1,0:T(8,128)(2,1)S(1)} %copy-done.29, f32[288,128]{1,0:T(8,128)S(1)} %copy-done.55), custom_call_target="tpu_custom_call" | custom-call | tf_op jit(solution)/shard_map/expert_slope/pallas_call | solution.py:50
  222.6 3.9 %expert_slope.9 = (bf16[288,512]{1,0:T(8,128)(2,1)S(1)}, f32[288,128]{1,0:T(8,128)S(1)}) custom-call(s32[2]{0:T(128)S(1)} %pad_add_fusion.me, bf16[512,512]{1,0:T(8,128)(2,1)S(1)} %get-tuple-element.83.q, bf16[288,512]{1,0:T(8,128)(2,1)S(1)} %copy-done.23, bf16[288,512]{1,0:T(8,128)(2,1)S(1)} %copy-done.25, f32[288,128]{1,0:T(8,128)S(1)} %get-tuple-element.91.cols), custom_call_target="tpu_custom_call" | custom-call | tf_op jit(solution)/shard_map/expert_slope/pallas_call | solution.py:50
  226.4 2.9 %collective-permute-done.14.part = bf16[288,1024]{1,0:T(8,128)(2,1)S(1)} collective-permute-done((bf16[288,1024]{1,0:T(8,128)(2,1)S(1)}, bf16[288,1024]{1,0:T(8,128)(2,1)S(1)}, u32[]{:S(2)}, u32[]{:S(2)}) %collective-permute-start.14) | collective-permute-done | bytes 589856 | tf_op jit(solution)/shard_map/ppermute | solution.py:467
  229.4 1.4 back.7
  230.8 3.5 %collective-permute-start.15 = (bf16[288,1024]{1,0:T(8,128)(2,1)}, bf16[288,1024]{1,0:T(8,128)(2,1)}, u32[]{:S(2)}, u32[]{:S(2)}) collective-permute-start(bf16[288,1024]{1,0:T(8,128)(2,1)} %back.7), channel_id=1, source_target_pairs={{0,224},{32,0},{64,32},{96,64},{128,96},{160,128},{192,160},{224,1... | collective-permute-start | bytes 1769480 | tf_op jit(solution)/shard_map/ppermute | solution.py:467
  234.3 1.4 back.5
  235.6 3.9 %expert_slope.8 = (bf16[288,512]{1,0:T(8,128)(2,1)S(1)}, f32[288,128]{1,0:T(8,128)S(1)}) custom-call(s32[2]{0:T(128)S(1)} %pad_add_fusion.me, bf16[512,512]{1,0:T(8,128)(2,1)S(1)} %get-tuple-element.83.q, bf16[288,512]{1,0:T(8,128)(2,1)S(1)} %copy-done.19, bf16[288,512]{1,0:T(8,128)(2,1)S(1)} %copy-done.21, f32[288,128]{1,0:T(8,128)S(1)} %copy-done.53), custom_call_target="tpu_custom_call" | custom-call | tf_op jit(solution)/shard_map/expert_slope/pallas_call | solution.py:50
  239.6 8.7 %weight_grads.1 = (f32[1024,512]{1,0:T(8,128)}, f32[8,2,1024]{2,1,0:T(2,128)}) custom-call(bf16[296,1024]{1,0:T(8,128)(2,1)S(1)} %unpack.1.x.refs_0_, bf16[296,1024]{1,0:T(8,128)(2,1)S(1)} %copy-done.8, bf16[296,1024]{1,0:T(8,128)(2,1)S(1)} %copy-done.11, bf16[296,1024]{1,0:T(8,128)(2,1)} %collective-permute-done.2.x.refs_3_, ...), custom_call_target="tpu_custom_call" | custom-call | tf_op jit(solution)/shard_map/weight_grads/pallas_call | solution.py:50
  248.2 3.9 %all-to-all-start.4 = ((f32[8,2,1024]{2,1,0:T(2,128)}), f32[8,2,1024]{2,1,0:T(2,128)S(1)}, u32[]{:S(2)}, u32[]{:S(2)}) async-start(f32[8,2,1024]{2,1,0:T(2,128)} %get-tuple-element.126), calls=%async_computation.4 | async-start | bytes 131072 | tf_op jit(solution)/shard_map/all_to_all | solution.py:389
  252.7 6.7 %all-to-all-done.4.small = f32[8,2,1024]{2,1,0:T(2,128)S(1)} async-done(((f32[8,2,1024]{2,1,0:T(2,128)}), f32[8,2,1024]{2,1,0:T(2,128)S(1)}, u32[]{:S(2)}, u32[]{:S(2)}) %all-to-all-start.4) | async-done | bytes 65568 | tf_op jit(solution)/shard_map/all_to_all | solution.py:389
  259.4 2.8 back_last.1
  262.2 7.9 %all-to-all-start.5 = ((bf16[32,8,1408]{2,1,0:T(8,128)(2,1)}), bf16[32,8,1408]{2,1,0:T(8,128)(2,1)S(1)}, u32[]{:S(2)}, u32[]{:S(2)}) async-start(bf16[32,8,1408]{2,1,0:T(8,128)(2,1)} %bitcast.13), calls=%async_computation.5 | async-start | bytes 1441792 | tf_op jit(solution)/shard_map/all_to_all | solution.py:389
  271.2 2.1 down_grad.1
  273.3 10.5 %all-to-all-done.5 = bf16[32,8,1408]{2,1,0:T(8,128)(2,1)S(1)} async-done(((bf16[32,8,1408]{2,1,0:T(8,128)(2,1)}), bf16[32,8,1408]{2,1,0:T(8,128)(2,1)S(1)}, u32[]{:S(2)}, u32[]{:S(2)}) %all-to-all-start.5) | async-done | bytes 720928 | tf_op jit(solution)/shard_map/all_to_all | solution.py:389
  283.8 1.9 final.1
  (174 shorter events, 26.1 us)
Async XLA Ops:
  3.7 77.4 %copy-start.69 = (f32[1024,32]{0,1:T(8,128)S(1)}, f32[1024,32]{0,1:T(8,128)}, u32[]{:S(2)}) copy-start(f32[1024,32]{0,1:T(8,128)} %param.13) | copy-start | bytes 393220
  3.7 77.5 %copy-start = (bf16[1,1024,512]{2,1,0:T(8,128)(2,1)S(1)}, bf16[1,1024,512]{2,1,0:T(8,128)(2,1)}, u32[]{:S(2)}) copy-start(bf16[1,1024,512]{2,1,0:T(8,128)(2,1)} %param.14) | copy-start | bytes 3145732
  4.7 57.7 %copy-start.50 = (bf16[288,212]{1,0:T(8,128)(2,1)}, bf16[288,212]{1,0:T(8,128)(2,1)S(1)}, u32[]{:S(2)}) copy-start(bf16[288,212]{1,0:T(8,128)(2,1)S(1)} %get-tuple-element.82.place) | copy-start | bytes 366340
  26.4 19.9 %collective-permute-start = (bf16[296,1024]{1,0:T(8,128)(2,1)S(1)}, bf16[296,1024]{1,0:T(8,128)(2,1)S(1)}, u32[]{:S(2)}, u32[]{:S(2)}) collective-permute-start(bf16[296,1024]{1,0:T(8,128)(2,1)S(1)} %unpack.1.x.refs_0_), channel_id=1, source_target_pairs={{0,32},{32,64},{64,96},{96,128},{128,160},{160,192},{192,224},{224... | collective-permute-start | bytes 1818632 | tf_op jit(solution)/shard_map/ppermute | solution.py:420
  28.1 19.0 %collective-permute-start.1 = (bf16[296,1024]{1,0:T(8,128)(2,1)S(1)}, bf16[296,1024]{1,0:T(8,128)(2,1)S(1)}, u32[]{:S(2)}, u32[]{:S(2)}) collective-permute-start(bf16[296,1024]{1,0:T(8,128)(2,1)S(1)} %unpack.1.x.refs_0_), channel_id=1, source_target_pairs={{0,224},{32,0},{64,32},{96,64},{128,96},{160,128},{192,160},{224,1... | collective-permute-start | bytes 1818632 | tf_op jit(solution)/shard_map/ppermute | solution.py:421
  46.3 16.2 %collective-permute-start.2 = (bf16[296,1024]{1,0:T(8,128)(2,1)S(1)}, bf16[296,1024]{1,0:T(8,128)(2,1)}, u32[]{:S(2)}, u32[]{:S(2)}) collective-permute-start(bf16[296,1024]{1,0:T(8,128)(2,1)S(1)} %collective-permute-done.x.refs_1_), channel_id=1, source_target_pairs={{0,32},{32,64},{64,96},{96,128},{128,160},{160,192},{192,224},{224... | collective-permute-start | bytes 1818632 | tf_op jit(solution)/shard_map/ppermute | solution.py:420
  47.1 15.3 %collective-permute-start.3 = (bf16[296,1024]{1,0:T(8,128)(2,1)S(1)}, bf16[296,1024]{1,0:T(8,128)(2,1)}, u32[]{:S(2)}, u32[]{:S(2)}) collective-permute-start(bf16[296,1024]{1,0:T(8,128)(2,1)S(1)} %collective-permute-done.1.x.refs_2_), channel_id=1, source_target_pairs={{0,224},{32,0},{64,32},{96,64},{128,96},{160,128},{192,160},{224,1... | collective-permute-start | bytes 1818632 | tf_op jit(solution)/shard_map/ppermute | solution.py:421
  62.5 15.4 %collective-permute-start.4 = (bf16[296,1024]{1,0:T(8,128)(2,1)}, bf16[296,1024]{1,0:T(8,128)(2,1)S(1)}, u32[]{:S(2)}, u32[]{:S(2)}) collective-permute-start(bf16[296,1024]{1,0:T(8,128)(2,1)} %collective-permute-done.2.x.refs_3_), channel_id=1, source_target_pairs={{0,32},{32,64},{64,96},{96,128},{128,160},{160,192},{192,224},{224... | collective-permute-start | bytes 1818632 | tf_op jit(solution)/shard_map/ppermute | solution.py:420
  62.5 15.5 %collective-permute-start.5 = (bf16[296,1024]{1,0:T(8,128)(2,1)}, bf16[296,1024]{1,0:T(8,128)(2,1)S(1)}, u32[]{:S(2)}, u32[]{:S(2)}) collective-permute-start(bf16[296,1024]{1,0:T(8,128)(2,1)} %collective-permute-done.3.x.refs_4_), channel_id=1, source_target_pairs={{0,224},{32,0},{64,32},{96,64},{128,96},{160,128},{192,160},{224,1... | collective-permute-start | bytes 1818632 | tf_op jit(solution)/shard_map/ppermute | solution.py:421
  65.7 17.1 %copy-start.7 = (bf16[296,1024]{1,0:T(8,128)(2,1)S(1)}, bf16[296,1024]{1,0:T(8,128)(2,1)}, u32[]{:S(2)}) copy-start(bf16[296,1024]{1,0:T(8,128)(2,1)} %copy-done.6) | copy-start | bytes 1818628
  77.8 18.3 %copy-start.2 = (bf16[296,1024]{1,0:T(8,128)(2,1)}, bf16[296,1024]{1,0:T(8,128)(2,1)S(1)}, u32[]{:S(2)}) copy-start(bf16[296,1024]{1,0:T(8,128)(2,1)S(1)} %collective-permute-done.4.x.refs_5_) | copy-start | bytes 1818628
  77.9 8.8 %copy-start.10 = (bf16[296,1024]{1,0:T(8,128)(2,1)S(1)}, bf16[296,1024]{1,0:T(8,128)(2,1)}, u32[]{:S(2)}) copy-start(bf16[296,1024]{1,0:T(8,128)(2,1)} %copy-done.9) | copy-start | bytes 1818628
  77.9 26.5 %collective-permute-start.6 = (bf16[144,1024]{1,0:T(8,128)(2,1)S(1)}, bf16[144,1024]{1,0:T(8,128)(2,1)S(1)}, u32[]{:S(2)}, u32[]{:S(2)}) collective-permute-start(bf16[144,1024]{1,0:T(8,128)(2,1)S(1)} %slice.8), channel_id=1, source_target_pairs={{0,32},{32,64},{64,96},{96,128},{128,160},{160,192},{192,224},{224... | collective-permute-start | bytes 884744 | tf_op jit(solution)/shard_map/ppermute | solution.py:423
  78.0 26.4 %collective-permute-start.7 = (bf16[152,1024]{1,0:T(8,128)(2,1)S(1)}, bf16[152,1024]{1,0:T(8,128)(2,1)S(1)}, u32[]{:S(2)}, u32[]{:S(2)}) collective-permute-start(bf16[152,1024]{1,0:T(8,128)(2,1)S(1)} %slice.9), channel_id=1, source_target_pairs={{0,224},{32,0},{64,32},{96,64},{128,96},{160,128},{192,160},{224,1... | collective-permute-start | bytes 933896 | tf_op jit(solution)/shard_map/ppermute | solution.py:424
  82.8 8.4 %copy-start.18 = (bf16[288,512]{1,0:T(8,128)(2,1)}, bf16[288,512]{1,0:T(8,128)(2,1)S(1)}, u32[]{:S(2)}) copy-start(bf16[288,512]{1,0:T(8,128)(2,1)S(1)} %get-tuple-element.84.act) | copy-start | bytes 884740
  82.8 8.4 %copy-start.20 = (bf16[288,512]{1,0:T(8,128)(2,1)}, bf16[288,512]{1,0:T(8,128)(2,1)S(1)}, u32[]{:S(2)}) copy-start(bf16[288,512]{1,0:T(8,128)(2,1)S(1)} %get-tuple-element.85.slope) | copy-start | bytes 884740
  82.8 8.4 %copy-start.52 = (f32[288,128]{1,0:T(8,128)}, f32[288,128]{1,0:T(8,128)S(1)}, u32[]{:S(2)}) copy-start(f32[288,128]{1,0:T(8,128)S(1)} %get-tuple-element.86.cols) | copy-start | bytes 442372
  88.3 11.6 %copy-start.22 = (bf16[288,512]{1,0:T(8,128)(2,1)}, bf16[288,512]{1,0:T(8,128)(2,1)S(1)}, u32[]{:S(2)}) copy-start(bf16[288,512]{1,0:T(8,128)(2,1)S(1)} %get-tuple-element.89.act) | copy-start | bytes 884740
  88.3 11.6 %copy-start.24 = (bf16[288,512]{1,0:T(8,128)(2,1)}, bf16[288,512]{1,0:T(8,128)(2,1)S(1)}, u32[]{:S(2)}) copy-start(bf16[288,512]{1,0:T(8,128)(2,1)S(1)} %get-tuple-element.90.slope) | copy-start | bytes 884740
  102.0 7.7 %copy-start.1 = (bf16[1,512,1024]{2,1,0:T(8,128)(2,1)S(1)}, bf16[1,512,1024]{2,1,0:T(8,128)(2,1)}, u32[]{:S(2)}) copy-start(bf16[1,512,1024]{2,1,0:T(8,128)(2,1)} %param.15) | copy-start | bytes 3145732
  154.1 21.9 %all-to-all-start.3 = ((bf16[32,16,1024]{2,1,0:T(8,128)(2,1)}), bf16[32,16,1024]{2,1,0:T(8,128)(2,1)}, u32[]{:S(2)}, u32[]{:S(2)}) async-start(bf16[32,16,1024]{2,1,0:T(8,128)(2,1)} %share.1), calls=%async_computation.3 | async-start | bytes 2097152 | tf_op jit(solution)/shard_map/all_to_all | solution.py:389
  176.0 10.0 %copy-start.47 = (bf16[288,512]{1,0:T(8,128)(2,1)S(1)}, bf16[288,512]{1,0:T(8,128)(2,1)}, u32[]{:S(2)}) copy-start(bf16[288,512]{1,0:T(8,128)(2,1)} %copy-done.46) | copy-start | bytes 884740
  176.0 10.0 %copy-start.49 = (bf16[288,512]{1,0:T(8,128)(2,1)S(1)}, bf16[288,512]{1,0:T(8,128)(2,1)}, u32[]{:S(2)}) copy-start(bf16[288,512]{1,0:T(8,128)(2,1)} %copy-done.48) | copy-start | bytes 884740
  176.0 10.0 %copy-start.65 = (f32[288,128]{1,0:T(8,128)S(1)}, f32[288,128]{1,0:T(8,128)}, u32[]{:S(2)}) copy-start(f32[288,128]{1,0:T(8,128)} %copy-done.64) | copy-start | bytes 442372
  176.0 16.0 %copy-start.43 = (bf16[288,512]{1,0:T(8,128)(2,1)S(1)}, bf16[288,512]{1,0:T(8,128)(2,1)}, u32[]{:S(2)}) copy-start(bf16[288,512]{1,0:T(8,128)(2,1)} %copy-done.42) | copy-start | bytes 884740
  176.0 16.0 %copy-start.45 = (bf16[288,512]{1,0:T(8,128)(2,1)S(1)}, bf16[288,512]{1,0:T(8,128)(2,1)}, u32[]{:S(2)}) copy-start(bf16[288,512]{1,0:T(8,128)(2,1)} %copy-done.44) | copy-start | bytes 884740
  176.0 16.0 %copy-start.63 = (f32[288,128]{1,0:T(8,128)S(1)}, f32[288,128]{1,0:T(8,128)}, u32[]{:S(2)}) copy-start(f32[288,128]{1,0:T(8,128)} %copy-done.62) | copy-start | bytes 442372
  186.0 9.9 %copy-start.39 = (bf16[288,512]{1,0:T(8,128)(2,1)S(1)}, bf16[288,512]{1,0:T(8,128)(2,1)}, u32[]{:S(2)}) copy-start(bf16[288,512]{1,0:T(8,128)(2,1)} %copy-done.38) | copy-start | bytes 884740
  186.0 9.9 %copy-start.41 = (bf16[288,512]{1,0:T(8,128)(2,1)S(1)}, bf16[288,512]{1,0:T(8,128)(2,1)}, u32[]{:S(2)}) copy-start(bf16[288,512]{1,0:T(8,128)(2,1)} %copy-done.40) | copy-start | bytes 884740
  186.0 9.9 %copy-start.61 = (f32[288,128]{1,0:T(8,128)S(1)}, f32[288,128]{1,0:T(8,128)}, u32[]{:S(2)}) copy-start(f32[288,128]{1,0:T(8,128)} %copy-done.60) | copy-start | bytes 442372
  190.4 9.3 %collective-permute-start.12 = (bf16[144,1024]{1,0:T(8,128)(2,1)S(1)}, bf16[144,1024]{1,0:T(8,128)(2,1)S(1)}, u32[]{:S(2)}, u32[]{:S(2)}) collective-permute-start(bf16[144,1024]{1,0:T(8,128)(2,1)S(1)} %get-tuple-element.125), channel_id=1, source_target_pairs={{0,224},{32,0},{64,32},{96,64},{128,96},{160,128},{192,160},{224,1... | collective-permute-start | bytes 884744 | tf_op jit(solution)/shard_map/ppermute | solution.py:467
  190.5 11.2 %collective-permute-start.8 = (bf16[144,1024]{1,0:T(8,128)(2,1)S(1)}, bf16[144,1024]{1,0:T(8,128)(2,1)S(1)}, u32[]{:S(2)}, u32[]{:S(2)}) collective-permute-start(bf16[144,1024]{1,0:T(8,128)(2,1)S(1)} %get-tuple-element.109), channel_id=1, source_target_pairs={{0,32},{32,64},{64,96},{96,128},{128,160},{160,192},{192,224},{224... | collective-permute-start | bytes 884744 | tf_op jit(solution)/shard_map/ppermute | solution.py:466
  200.3 14.2 %collective-permute-start.13 = (bf16[288,1024]{1,0:T(8,128)(2,1)S(1)}, bf16[288,1024]{1,0:T(8,128)(2,1)S(1)}, u32[]{:S(2)}, u32[]{:S(2)}) collective-permute-start(bf16[288,1024]{1,0:T(8,128)(2,1)S(1)} %back_half.3), channel_id=1, source_target_pairs={{0,224},{32,0},{64,32},{96,64},{128,96},{160,128},{192,160},{224,1... | collective-permute-start | bytes 1769480 | tf_op jit(solution)/shard_map/ppermute | solution.py:467
  202.2 15.8 %collective-permute-start.9 = (bf16[288,1024]{1,0:T(8,128)(2,1)S(1)}, bf16[288,1024]{1,0:T(8,128)(2,1)S(1)}, u32[]{:S(2)}, u32[]{:S(2)}) collective-permute-start(bf16[288,1024]{1,0:T(8,128)(2,1)S(1)} %back_half.2), channel_id=1, source_target_pairs={{0,32},{32,64},{64,96},{96,128},{128,160},{160,192},{192,224},{224... | collective-permute-start | bytes 1769480 | tf_op jit(solution)/shard_map/ppermute | solution.py:466
  215.1 14.2 %collective-permute-start.14 = (bf16[288,1024]{1,0:T(8,128)(2,1)S(1)}, bf16[288,1024]{1,0:T(8,128)(2,1)S(1)}, u32[]{:S(2)}, u32[]{:S(2)}) collective-permute-start(bf16[288,1024]{1,0:T(8,128)(2,1)S(1)} %back.6), channel_id=1, source_target_pairs={{0,224},{32,0},{64,32},{96,64},{128,96},{160,128},{192,160},{224,1... | collective-permute-start | bytes 1769480 | tf_op jit(solution)/shard_map/ppermute | solution.py:467
  218.6 15.7 %collective-permute-start.10 = (bf16[288,1024]{1,0:T(8,128)(2,1)S(1)}, bf16[288,1024]{1,0:T(8,128)(2,1)S(1)}, u32[]{:S(2)}, u32[]{:S(2)}) collective-permute-start(bf16[288,1024]{1,0:T(8,128)(2,1)S(1)} %back.4), channel_id=1, source_target_pairs={{0,32},{32,64},{64,96},{96,128},{128,160},{160,192},{192,224},{224... | collective-permute-start | bytes 1769480 | tf_op jit(solution)/shard_map/ppermute | solution.py:466
  230.8 8.8 %copy-start.3 = (bf16[296,1024]{1,0:T(8,128)(2,1)S(1)}, bf16[296,1024]{1,0:T(8,128)(2,1)}, u32[]{:S(2)}) copy-start(bf16[296,1024]{1,0:T(8,128)(2,1)} %copy-done.2) | copy-start | bytes 1818628
  230.8 8.8 %copy-start.5 = (bf16[296,1024]{1,0:T(8,128)(2,1)S(1)}, bf16[296,1024]{1,0:T(8,128)(2,1)}, u32[]{:S(2)}) copy-start(bf16[296,1024]{1,0:T(8,128)(2,1)} %copy-done.4) | copy-start | bytes 1818628
  230.8 8.8 %copy-start.8 = (bf16[296,1024]{1,0:T(8,128)(2,1)S(1)}, bf16[296,1024]{1,0:T(8,128)(2,1)}, u32[]{:S(2)}) copy-start(bf16[296,1024]{1,0:T(8,128)(2,1)} %copy-done.6) | copy-start | bytes 1818628
  230.8 8.8 %copy-start.11 = (bf16[296,1024]{1,0:T(8,128)(2,1)S(1)}, bf16[296,1024]{1,0:T(8,128)(2,1)}, u32[]{:S(2)}) copy-start(bf16[296,1024]{1,0:T(8,128)(2,1)} %copy-done.9) | copy-start | bytes 1818628
  230.8 28.6 %collective-permute-start.15 = (bf16[288,1024]{1,0:T(8,128)(2,1)}, bf16[288,1024]{1,0:T(8,128)(2,1)}, u32[]{:S(2)}, u32[]{:S(2)}) collective-permute-start(bf16[288,1024]{1,0:T(8,128)(2,1)} %back.7), channel_id=1, source_target_pairs={{0,224},{32,0},{64,32},{96,64},{128,96},{160,128},{192,160},{224,1... | collective-permute-start | bytes 1769480 | tf_op jit(solution)/shard_map/ppermute | solution.py:467
  235.6 23.8 %collective-permute-start.11 = (bf16[288,1024]{1,0:T(8,128)(2,1)}, bf16[288,1024]{1,0:T(8,128)(2,1)}, u32[]{:S(2)}, u32[]{:S(2)}) collective-permute-start(bf16[288,1024]{1,0:T(8,128)(2,1)} %back.5), channel_id=1, source_target_pairs={{0,32},{32,64},{64,96},{96,128},{128,160},{160,192},{192,224},{224... | collective-permute-start | bytes 1769480 | tf_op jit(solution)/shard_map/ppermute | solution.py:466
  248.2 11.2 %all-to-all-start.4 = ((f32[8,2,1024]{2,1,0:T(2,128)}), f32[8,2,1024]{2,1,0:T(2,128)S(1)}, u32[]{:S(2)}, u32[]{:S(2)}) async-start(f32[8,2,1024]{2,1,0:T(2,128)} %get-tuple-element.126), calls=%async_computation.4 | async-start | bytes 131072 | tf_op jit(solution)/shard_map/all_to_all | solution.py:389
  252.7 17.4 %copy-start.15 = (bf16[512,1024]{1,0:T(8,128)(2,1)S(1)}, bf16[512,1024]{1,0:T(8,128)(2,1)}, u32[]{:S(2)}) copy-start(bf16[512,1024]{1,0:T(8,128)(2,1)} %copy-done.14) | copy-start | bytes 3145732
  262.2 21.6 %copy-start.51 = (bf16[288,212]{1,0:T(8,128)(2,1)S(1)}, bf16[288,212]{1,0:T(8,128)(2,1)}, u32[]{:S(2)}) copy-start(bf16[288,212]{1,0:T(8,128)(2,1)} %copy-done.50) | copy-start | bytes 366340
  262.2 21.6 %copy-start.67 = (f32[1024]{0:T(1024)S(1)}, f32[1024]{0:T(1024)}, u32[]{:S(2)}) copy-start(f32[1024]{0:T(1024)} %param.12) | copy-start | bytes 12292
  262.2 21.6 %all-to-all-start.5 = ((bf16[32,8,1408]{2,1,0:T(8,128)(2,1)}), bf16[32,8,1408]{2,1,0:T(8,128)(2,1)S(1)}, u32[]{:S(2)}, u32[]{:S(2)}) async-start(bf16[32,8,1408]{2,1,0:T(8,128)(2,1)} %bitcast.13), calls=%async_computation.5 | async-start | bytes 1441792 | tf_op jit(solution)/shard_map/all_to_all | solution.py:389
  270.1 13.7 %copy-start.13 = (bf16[1,212,1024]{2,1,0:T(8,128)(2,1)S(1)}, bf16[1,212,1024]{2,1,0:T(8,128)(2,1)}, u32[]{:S(2)}) copy-start(bf16[1,212,1024]{2,1,0:T(8,128)(2,1)} %param.9) | copy-start | bytes 1302532
  (41 other events, 98.7 us)

commit v2 on v1

--- a/solution.py
+++ b/solution.py
@@ -45,8 +45,8 @@
     return lax.broadcasted_iota(I32, shape, axis)
 
 
-def run(kernel, outs, *args, smem=0, scratch=(), name=None):
-    specs = [SM] * smem + [VM] * (len(args) - smem)
+def run(kernel, outs, *args, smem=0, scratch=(), name=None, limit=6, stage=False):
+    specs = [SM] * smem + [pl.BlockSpec() if stage else VM] * (len(args) - smem)
     return pl.pallas_call(
         kernel,
         out_shape=outs,
@@ -54,7 +54,7 @@
         out_specs=jax.tree.map(lambda _: VM, outs),
         scratch_shapes=scratch,
         name=name,
-        compiler_params=pltpu.CompilerParams(vmem_limit_bytes=32 * 1024 * 1024),
+        compiler_params=pltpu.CompilerParams(vmem_limit_bytes=limit * 1024 * 1024),
     )(*args)
 
 
@@ -130,28 +130,36 @@
 CHUNK = 32
 
 
-def forward_kernel(x, wu, router, act, slope, cols, pooled, pre, mixed):
+def forward_math(x, wu, router, act, slope, cols, pooled, pre, mixed):
     pre[...] = mm(x[:ROWS], wu[...])
     meta = x[ROWS:, :LANES].astype(F32)
     pt_row = meta[0:1]
-    div_row = meta[1:2]
+
+    def gates(c, _):
+        at = pl.ds(pl.multiple_of(c * CHUNK, CHUNK), CHUNK)
+        prod = x[at, :].astype(F32) * router[...]
+        t = prod[:, :128]
+        for k in range(1, 8):
+            t = t + prod[:, 128 * k : 128 * (k + 1)]
+        cols[at, :] = t
+        return 0
+
+    lax.fori_loop(0, ROWS // CHUNK, gates, 0)
+    gate = jax.nn.sigmoid(jnp.sum(cols[...], axis=1, keepdims=True))
+    diag = io((ROWS, LANES), 1) == io((ROWS, LANES), 0)
+    div = jnp.sum(jnp.where(diag, meta[1:2], 0.0), axis=1, keepdims=True)
+    pt = jnp.sum(jnp.where(diag, pt_row, 0.0), axis=1, keepdims=True)
+    lane = io((ROWS, 128), 1)
+    cols[...] = jnp.where(lane == 0, gate / div, jnp.where(lane == 1, 1.0 - gate, jnp.where(lane == 2, pt, 0.0)))
 
     def step(c, _):
         at = pl.ds(pl.multiple_of(c * CHUNK, CHUNK), CHUNK)
-        xc = x[at, :].astype(F32)
-        gate = jax.nn.sigmoid(jnp.sum(xc * router[...], axis=1, keepdims=True))
-        diag = io((CHUNK, LANES), 1) == io((CHUNK, LANES), 0) + c * CHUNK
-        div = jnp.sum(jnp.where(diag, div_row, 0.0), axis=1, keepdims=True)
-        pt = jnp.sum(jnp.where(diag, pt_row, 0.0), axis=1, keepdims=True)
-        scaled = gate / div
         p = pre[at, :]
         phi = 0.5 * (1.0 + lax.erf(p * 0.7071067811865476))
         a = (p * phi).astype(BF)
         act[at, :] = a
         slope[at, :] = (phi + p * jnp.exp(-0.5 * p * p) * 0.3989422804014327).astype(BF)
-        mixed[at, :] = (scaled * a.astype(F32)).astype(BF)
-        lane = io((CHUNK, 128), 1)
-        cols[at, :] = jnp.where(lane == 0, scaled, jnp.where(lane == 1, 1.0 - gate, jnp.where(lane == 2, pt, 0.0)))
+        mixed[at, :] = (cols[at, 0:1] * a.astype(F32)).astype(BF)
         return 0
 
     lax.fori_loop(0, ROWS // CHUNK, step, 0)
@@ -159,16 +167,36 @@
     pooled[...] = mm(sel, mixed[...]).astype(BF)
 
 
+def forward_kernel(x, wu, router, act, slope, cols, pooled, pre, mixed):
+    forward_math(x, wu, router, act, slope, cols, pooled, pre, mixed)
+
+
+def forward_join_kernel(top, low, wu, router, act, slope, cols, pooled, x, pre, mixed):
+    x[:CUT] = top[...]
+    x[CUT:] = low[...]
+    forward_math(x, wu, router, act, slope, cols, pooled, pre, mixed)
+
+
+FORWARD_OUT = (shape(ROWS, FD), shape(ROWS, FD), shape(ROWS, 128, dtype=F32), shape(LOCAL, FD))
+FORWARD_SCRATCH = [pltpu.VMEM((ROWS, FD), F32), pltpu.VMEM((ROWS, FD), BF)]
+
+
 def forward_block(x, wu, router):
-    return run(
-        forward_kernel,
-        (shape(ROWS, FD), shape(ROWS, FD), shape(ROWS, 128, dtype=F32), shape(LOCAL, FD)),
-        x,
+    return (x,) + tuple(run(forward_kernel, FORWARD_OUT, x, wu, router, scratch=FORWARD_SCRATCH, name="expert_forward"))
+
+
+def forward_join(top, low, wu, router):
+    out = run(
+        forward_join_kernel,
+        FORWARD_OUT + (shape(HEIGHT, D),),
+        top,
+        low,
         wu,
         router,
-        scratch=[pltpu.VMEM((ROWS, FD), F32), pltpu.VMEM((ROWS, FD), BF)],
-        name="expert_forward",
-    )
+        scratch=FORWARD_SCRATCH,
+        name="expert_forward_join",
+    )
+    return (out[4],) + tuple(out[:4])
 
 
 def part_kernel(offsets, me, *refs):
@@ -178,7 +206,7 @@
     p = io((PT, LOCAL), 1)
     for ref, off in zip(refs[:NDP], offsets):
         src = (me[0] + off) % NDP
-        perm = (g == (p // 2) * (2 * NDP) + src * 2 + p % 2).astype(BF)
+        perm = (g == (p // 2) * (2 * NDP) + (p % 2) * NDP + src).astype(BF)
         term = mm(perm, ref[...])
         total = term if total is None else total + term
     pooled[...] = total.astype(BF)
@@ -188,8 +216,7 @@
 def column_kernel(me, got, means, out):
     s = jnp.sum(got[...].astype(F32), axis=0)
     row = io((2 * NDP, 1), 0)
-    own = row // 2 == me[0]
-    s = s + jnp.where(own & (row % 2 == 0), means[0:1], 0.0) + jnp.where(own & (row % 2 == 1), means[1:2], 0.0)
+    s = s + jnp.where(row == me[0], means[0:1], 0.0) + jnp.where(row == me[0] + NDP, means[1:2], 0.0)
     out[...] = jnp.broadcast_to(s.astype(BF)[None], (NDP, 2 * NDP, D))
 
 
@@ -198,84 +225,74 @@
     out[...] = jnp.broadcast_to(s.astype(BF)[None], (NEX, 2 * NDP, D))
 
 
-def loss_kernel(me, scale, bias, emb, wd, loss, d_emb, dy, q, dots, inv_col, high, low, grads):
-    e = emb[...]
-    dots[...] = mm(e, e, ((1,), (1,)))
+def loss_kernel(me, scale, bias, emb, wd, loss, d_emb, dy, q, grads):
+    n = PT // 2
+    u = emb[:, :NDP].reshape(n, D)
+    v = emb[:, NDP:].reshape(n, D)
+    dots = mm(u, v, ((1,), (1,)))
+    i = io((n, n), 0)
+    j = io((n, n), 1)
+    same = i == j
+
+    def norms(a):
+        on = jnp.where(same, mm(a, a, ((1,), (1,))), 0.0)
+        col = 1.0 / jnp.sqrt(jnp.sum(on, axis=1, keepdims=True) / D + EPS)
+        row = 1.0 / jnp.sqrt(jnp.sum(on, axis=0, keepdims=True) / D + EPS)
+        return col, row
+
+    iu, iu_row = norms(u)
+    iv, iv_row = norms(v)
     to_unit = scale[0] / D
-    step_rows = 64
-    steps = PT // step_rows
-
-    def norms(c, row_sum):
-        at = pl.ds(pl.multiple_of(c * step_rows, step_rows), step_rows)
-        diag = io((step_rows, PT), 1) == io((step_rows, PT), 0) + c * step_rows
-        on = jnp.where(diag, dots[at, :], 0.0)
-        inv = 1.0 / jnp.sqrt(jnp.sum(on, axis=1, keepdims=True) / D + EPS)
-        inv_col[at, :] = jnp.broadcast_to(inv, (step_rows, 128))
-        return row_sum + jnp.sum(on, axis=0, keepdims=True)
-
-    squares = lax.fori_loop(0, steps, norms, jnp.zeros((1, PT), F32))
-    inv_row = 1.0 / jnp.sqrt(squares / D + EPS)
-
-    def terms(c, total):
-        at = pl.ds(pl.multiple_of(c * step_rows, step_rows), step_rows)
-        i = io((step_rows, PT), 0) + c * step_rows
-        j = io((step_rows, PT), 1)
-        same = i // 2 == j // 2
-        sign = jnp.where(same, 1.0, -1.0)
-        cross = i % 2 != j % 2
-        z = sign * (dots[at, :] * to_unit * inv_col[at, 0:1] * inv_row + bias[0])
-        t = jnp.exp(-jnp.abs(z))
-        soft = jnp.maximum(-z, 0.0) + jnp.log1p(t)
-        sig = jnp.where(z >= 0.0, t, 1.0) / (1.0 + t)
-        coef = jnp.where(cross, (-LOSS_SCALE / (PT // 2)) * sign * sig, 0.0) * inv_row * to_unit
-        hi = coef.astype(BF)
-        high[at, :] = hi
-        low[at, :] = (coef - hi.astype(F32)).astype(BF)
-        return total + jnp.sum(jnp.where(cross & (i % 2 == 0), soft, 0.0), axis=0, keepdims=True)
-
-    total = lax.fori_loop(0, steps, terms, jnp.zeros((1, PT), F32))
-    loss[...] = jnp.sum(total, axis=1, keepdims=True) / (PT // 2)
-    grads[...] = mm(high[...], e) + mm(low[...], e)
-
-    def project(c, _):
-        at = pl.ds(pl.multiple_of(c * step_rows, step_rows), step_rows)
-        inv = inv_col[at, 0:1]
-        unit = emb[at, :].astype(F32) * inv
-        dw = grads[at, :]
-        res = (dw - unit * (jnp.sum(dw * unit, axis=1, keepdims=True) / D)) * inv
-        grads[at, :] = res
-        d_emb[at, :] = res.astype(BF)
-        return 0
-
-    lax.fori_loop(0, steps, project, 0)
-    first = (me[1] * NDP + me[0]) * 2
-    base = pl.multiple_of((first // 8) * 8, 8)
-    near = grads[pl.ds(base, 8), :]
-    row = io((8, 1), 0)
-    dy[0:1] = jnp.sum(jnp.where(row == first % 8, near, 0.0), axis=0, keepdims=True)
-    dy[1:2] = jnp.sum(jnp.where(row == first % 8 + 1, near, 0.0), axis=0, keepdims=True)
-    raw = mm(d_emb[...], wd[...], ((1,), (1,))).astype(BF)
-    i = io((PT, PT), 0)
-    at = (i % LOCAL) // 2 * (2 * NDP) + (i // LOCAL) * 2 + i % 2
+    sign = jnp.where(same, 1.0, -1.0)
+    z = sign * (dots * to_unit * iu * iv_row + bias[0])
+    t = jnp.exp(-jnp.abs(z))
+    soft = jnp.maximum(-z, 0.0) + jnp.log1p(t)
+    loss[...] = jnp.sum(jnp.sum(soft, axis=0, keepdims=True), axis=1, keepdims=True) / n
+    coef = (-LOSS_SCALE / n) * sign * (jnp.where(z >= 0.0, t, 1.0) / (1.0 + t)) * to_unit
+    for_u = coef * iv_row
+    for_v = coef * iu
+
+    def halves(c):
+        hi = c.astype(BF)
+        return hi, (c - hi.astype(F32)).astype(BF)
+
+    u_hi, u_lo = halves(for_u)
+    v_hi, v_lo = halves(for_v)
+    u_dot = jnp.sum(for_u * dots, axis=1, keepdims=True)
+    v_dot_row = jnp.sum(for_v * dots, axis=0, keepdims=True)
+    v_dot = jnp.sum(jnp.where(same, v_dot_row, 0.0), axis=1, keepdims=True)
+    grads[0] = (mm(u_hi, v) + mm(u_lo, v)) * iu - u.astype(F32) * (iu * iu * iu * u_dot / D)
+    first = ((0,), (0,))
+    grads[1] = (mm(v_hi, u, first) + mm(v_lo, u, first)) * iv - v.astype(F32) * (iv * iv * iv * v_dot / D)
+    d_emb[:, :NDP] = grads[0].astype(BF).reshape(NEX, NDP, D)
+    d_emb[:, NDP:] = grads[1].astype(BF).reshape(NEX, NDP, D)
+    raw = mm(d_emb[...].reshape(PT, D), wd[...], ((1,), (1,))).astype(BF)
+    r = io((PT, PT), 0)
+    at = (r % LOCAL) // 2 * (2 * NDP) + (r % 2) * NDP + r // LOCAL
     perm = (io((PT, PT), 1) == at).astype(BF)
     q[...] = mm(perm, raw).astype(BF)
-
-
-def slope_kernel(off, me, q, act, slope, cols, dpre, dgl):
+    row = io((NDP, 1), 0)
+    near = pl.ds(pl.multiple_of(me[1] * NDP, NDP), NDP)
+    for kind in range(2):
+        dy[kind : kind + 1] = jnp.sum(jnp.where(row == me[0], grads[kind, near, :], 0.0), axis=0, keepdims=True)
+
+
+def slope_kernel(off, me, q, act, slope, cols, dpre, dgl, dact, partial):
     src = (me[0] + off) % NDP
     qb = q[pl.ds(pl.multiple_of(src * LOCAL, LOCAL), LOCAL), :]
+    pick = (io((ROWS, LOCAL), 1).astype(F32) == cols[:, 2:3]).astype(BF)
+    dact[...] = mm(pick, qb)
 
     def step(c, _):
         at = pl.ds(pl.multiple_of(c * CHUNK, CHUNK), CHUNK)
-        col = cols[at, :]
-        pick = (io((CHUNK, LOCAL), 1).astype(F32) == col[:, 2:3]).astype(BF)
-        dact = mm(pick, qb) * col[:, 0:1]
-        dpre[at, :] = (dact * slope[at, :].astype(F32)).astype(BF)
-        dots = jnp.sum(dact * act[at, :].astype(F32), axis=1, keepdims=True) * col[:, 1:2]
-        dgl[at, :] = jnp.broadcast_to(dots, (CHUNK, 128))
+        da = dact[at, :] * cols[at, 0:1]
+        dpre[at, :] = (da * slope[at, :].astype(F32)).astype(BF)
+        prod = da * act[at, :].astype(F32)
+        partial[at, :] = prod[:, :128] + prod[:, 128:256] + prod[:, 256:384] + prod[:, 384:]
         return 0
 
     lax.fori_loop(0, ROWS // CHUNK, step, 0)
+    dgl[...] = jnp.broadcast_to(jnp.sum(partial[...], axis=1, keepdims=True) * cols[:, 1:2], (ROWS, 128))
 
 
 def slope_block(off, me, q, saved):
@@ -289,6 +306,7 @@
         slope,
         cols,
         smem=1,
+        scratch=[pltpu.VMEM((ROWS, FD), F32), pltpu.VMEM((ROWS, 128), F32)],
         name="expert_slope",
     )
 
@@ -361,7 +379,7 @@
 
 
 def down_kernel(pooled, d_emb, out):
-    out[...] = mm(pooled[...], d_emb[...], ((0,), (0,)))
+    out[...] = mm(pooled[...], d_emb[...].reshape(PT, D), ((0,), (0,)))
 
 
 def final_kernel(length, tok, gain, place, got, dy, grad_tokens, grad_router, gain_grad):
@@ -385,6 +403,21 @@
         gain_grad[:, at_k] = jnp.sum(piece[:, 128:], axis=0, keepdims=True) / gain[:, at_k]
 
 
+def weight_grads(xs, slopes, offsets, wu, router_row):
+    return run(
+        weight_kernel,
+        (shape(D, FD, dtype=F32), shape(NDP, 2, D, dtype=F32)),
+        *[xs[off] for off in offsets],
+        *[slopes[off][0] for off in offsets],
+        *[slopes[off][1] for off in offsets],
+        wu,
+        router_row,
+        scratch=[pltpu.VMEM((D, FD), F32)],
+        name="weight_grads",
+        limit=12,
+    )
+
+
 def exchange(value, axis):
     return lax.all_to_all(value, axis, split_axis=0, concat_axis=0, tiled=True)
 
@@ -406,6 +439,7 @@
         gain_row,
         smem=1,
         name="front",
+        stage=True,
     )
     got = exchange(send.reshape(NEX, 8, SEND_W), "expert").reshape(MAIN, SEND_W)
     own = run(unpack_kernel, shape(HEIGHT, D), got, name="unpack")
@@ -415,16 +449,25 @@
     half = NDP // 2
     router_row = jnp.sum(jnp.where(jnp.arange(NEX, dtype=I32)[None, :] == me_ex, router, 0.0), axis=1).reshape(1, D)
     r, l = own, own
-    xs = {0: own}
+    saved = {}
+    ready = [(0, own)]
     for k in range(1, half):
-        r = lax.ppermute(r, "dp", right)
-        l = lax.ppermute(l, "dp", left)
-        xs[-k], xs[k] = r, l
-    r = lax.ppermute(r[:CUT], "dp", right)
-    l = lax.ppermute(l[CUT:], "dp", left)
-    xs[half] = jnp.concatenate([r, l], axis=0)
-    offsets = list(xs)
-    saved = {off: (x,) + tuple(forward_block(x, wu, router_row)) for off, x in xs.items()}
+        nr = lax.ppermute(r, "dp", right)
+        nl = lax.ppermute(l, "dp", left)
+        for off, x in ready:
+            saved[off] = forward_block(x, wu, router_row)
+        flat = [saved[off] for off, _ in ready]
+        r, l, flat = lax.optimization_barrier((nr, nl, flat))
+        for (off, _), value in zip(ready, flat):
+            saved[off] = value
+        ready = [(-k, r), (k, l)]
+    top = lax.ppermute(r[:CUT], "dp", right)
+    low = lax.ppermute(l[CUT:], "dp", left)
+    for off, x in ready:
+        saved[off] = forward_block(x, wu, router_row)
+    saved[half] = forward_join(top, low, wu, router_row)
+    offsets = list(saved)
+    xs = {off: saved[off][0] for off in offsets}
     part, pooled = run(
         functools.partial(part_kernel, offsets),
         (shape(PT, D), shape(PT, FD)),
@@ -438,23 +481,18 @@
     column = run(column_kernel, shape(NDP, 2 * NDP, D), me, part, means, smem=1, name="column")
     column = exchange(column, "dp")
     shared = run(share_kernel, shape(NEX, 2 * NDP, D), column, name="share")
-    emb = exchange(shared, "expert").reshape(PT, D)
+    emb = exchange(shared, "expert")
     loss, d_emb, dy, q = run(
         loss_kernel,
-        (shape(1, 1, dtype=F32), shape(PT, D), shape(2, D, dtype=F32), shape(PT, FD)),
+        (shape(1, 1, dtype=F32), shape(NEX, 2 * NDP, D), shape(2, D, dtype=F32), shape(PT, FD)),
         me,
         logit_scale,
         logit_bias,
         emb,
         wd,
         smem=3,
-        scratch=[
-            pltpu.VMEM((PT, PT), F32),
-            pltpu.VMEM((PT, 128), F32),
-            pltpu.VMEM((PT, PT), BF),
-            pltpu.VMEM((PT, PT), BF),
-            pltpu.VMEM((PT, D), F32),
-        ],
+        scratch=[pltpu.VMEM((2, PT // 2, D), F32)],
+        limit=16,
         name="pair_loss",
     )
 
@@ -462,28 +500,24 @@
     r, l = run(back_first_kernel, (shape(CUT, D), shape(CUT, D)), *slopes[half], wu, router_row, name="back_first")
     for off in (half - 1, 1 - half, 2, -2, 1, -1, 0):
         slopes[off] = slope_block(off, me, q, saved[off])
+    small = None
     for k in range(half - 1, -1, -1):
         r = lax.ppermute(r, "dp", right)
         l = lax.ppermute(l, "dp", left)
         if k == half - 1:
+            r, l, slopes = lax.optimization_barrier((r, l, slopes))
             r = run(functools.partial(back_half_kernel, True), shape(ROWS, D), *slopes[k], wu, router_row, r, name="back_half")
             l = run(functools.partial(back_half_kernel, False), shape(ROWS, D), *slopes[-k], wu, router_row, l, name="back_half")
         elif k > 0:
+            if k == half - 2:
+                grad_up, small = weight_grads(xs, slopes, offsets, wu, router_row)
+                r, l, small = lax.optimization_barrier((r, l, small))
+            else:
+                small = exchange(small, "dp")
+                r, l, small = lax.optimization_barrier((r, l, small))
             r = run(back_kernel, shape(ROWS, D), *slopes[k], wu, router_row, r, name="back")
             l = run(back_kernel, shape(ROWS, D), *slopes[-k], wu, router_row, l, name="back")
-    grad_up, small = run(
-        weight_kernel,
-        (shape(D, FD, dtype=F32), shape(NDP, 2, D, dtype=F32)),
-        *[xs[off] for off in offsets],
-        *[slopes[off][0] for off in offsets],
-        *[slopes[off][1] for off in offsets],
-        wu,
-        router_row,
-        scratch=[pltpu.VMEM((D, FD), F32)],
-        name="weight_grads",
-    )
     grad_down = run(down_kernel, shape(FD, D, dtype=F32), pooled, d_emb, name="down_grad")
-    small = exchange(small, "dp")
     own_back = run(back_own_kernel, shape(ROWS, D, dtype=F32), *slopes[0], wu, router_row, name="back_own")
     send = run(back_last_kernel, shape(MAIN, BACK_W), own_back, r, l, small, name="back_last")
     got = exchange(send.reshape(NEX, 8, BACK_W), "expert").reshape(MAIN, BACK_W)

time: 286 us -> 259 us (0.906)
  Pallas kernels: 82.2 us -> 55.8 us
  blocking collectives: 60.9 us -> 75.2 us
  waiting for transfers between devices: 78.1 us -> 68.6 us
  starting transfers between devices: 41.1 us -> 34.5 us
    ppermute x7 -> x4, waiting for transfers between devices: 38.2 us -> 2.56 us  [body(): r = lax.ppermute(r, 'dp', right)]
    pallas_call x34, Pallas kernels: 82.2 us -> 55.8 us  [run(): pl.pallas_call(kernel, out_shape=outs, in_specs=specs, out_specs=jax.tree...]
    ppermute x2 -> x8, waiting for transfers between devices: 0.01 us -> 24.5 us  [the longest x3 13.9 us: body(): nr = lax.ppermute(r, 'dp', right)]
    ppermute x7 -> x4, starting transfers between devices: 17.7 us -> 2.89 us  [body(): l = lax.ppermute(l, 'dp', left)]
    all_to_all x3 -> x4, blocking collectives: 60.9 us -> 75.2 us  [exchange(): return lax.all_to_all(value, axis, split_axis=0, concat_axis=0, tiled=True)]
    ppermute x2 -> x8, starting transfers between devices: 3.05 us -> 13.4 us  [the longest x3 11 us: body(): nl = lax.ppermute(l, 'dp', left)]
    ppermute x7 -> x4, waiting for transfers between devices: 7.02 us -> 14.3 us  [body(): l = lax.ppermute(l, 'dp', left)]
    all_to_all x3 -> x2, waiting for transfers between devices: 32.9 us -> 27.2 us  [exchange(): return lax.all_to_all(value, axis, split_axis=0, concat_axis=0, tiled=True)]
  transfers between devices with their start and end apart: 19 -> 18, of which waited for: 8 -> 10; matrix products, arithmetic and copies ran while one was open for 0% -> 0% of each run, Pallas kernels for 20% -> 14%
where the time goes in v2:
time: 259 us
  blocking collectives  75.2 us (29%)
  waiting for transfers between devices  68.6 us (26%)
  Pallas kernels  55.8 us (22%)
  starting transfers between devices  34.5 us (13%)
  local copies, waits for them, and re-layouts  20.5 us (8%)
  between operations  3.64 us (1%)
    all_to_all x4, blocking collectives, exchange(): return lax.all_to_all(value, axis, split_axis=0, concat_axis=0, tiled=True)  75.2 us
    pallas_call x34, Pallas kernels, run(): pl.pallas_call(kernel, out_shape=outs, in_specs=specs, out_specs=jax.tree...  55.8 us
    all_to_all x2, waiting for transfers between devices, exchange(): return lax.all_to_all(value, axis, split_axis=0, concat_axis=0, tiled=True)  27.2 us
    unnamed x162, local copies, waits for them, and re-layouts  19 us
    ppermute x4, waiting for transfers between devices, body(): l = lax.ppermute(l, 'dp', left)  14.3 us
    ppermute x3, waiting for transfers between devices, body(): nr = lax.ppermute(r, 'dp', right)  13.9 us
    all_to_all x2, starting transfers between devices, exchange(): return lax.all_to_all(value, axis, split_axis=0, concat_axis=0, tiled=True)  13.4 us
    ppermute x3, starting transfers between devices, body(): nl = lax.ppermute(l, 'dp', left)  11 us
  transfers between devices with their start and end apart: 18, of which 10 were waited for; matrix products, arithmetic and copies ran while one was open for 0% of the time, Pallas kernels for 14%

profile of v2, /device:TPU:1, one launch (start us, length us, event | category | flops | bytes accessed | tf_op | source)
XLA Modules:
  0.0 258.5 jit_solution(17142768806294061329)
XLA Ops:
  3.8 1.1 front.1
  4.8 21.3 %all_to_all.30 = bf16[32,8,1280]{2,1,0:T(8,128)(2,1)S(1)} all-to-all(bf16[32,8,1280]{2,1,0:T(8,128)(2,1)S(1)} %bitcast.60), channel_id=1, replica_groups=mesh['dp'=8,'expert'=32] {'expert'}, dimensions={0} | all-to-all | bytes 1310720 | tf_op jit(solution)/shard_map/all_to_all | solution.py:422
  26.5 5.6 %collective-permute-start.1 = (bf16[296,1024]{1,0:T(8,128)(2,1)S(1)}, bf16[296,1024]{1,0:T(8,128)(2,1)S(1)}, u32[]{:S(2)}, u32[]{:S(2)}) collective-permute-start(bf16[296,1024]{1,0:T(8,128)(2,1)S(1)} %unpack.1.x.refs_0_), channel_id=1, source_target_pairs={{0,224},{32,0},{64,32},{96,64},{128,96},{160,128},{192,160},{224,1... | collective-permute-start | bytes 1818632 | tf_op jit(solution)/shard_map/ppermute | solution.py:456
  32.3 1.7 expert_forward.7
  34.7 10.7 %collective-permute-done.1.x.refs_2_ = bf16[296,1024]{1,0:T(8,128)(2,1)S(1)} collective-permute-done((bf16[296,1024]{1,0:T(8,128)(2,1)S(1)}, bf16[296,1024]{1,0:T(8,128)(2,1)S(1)}, u32[]{:S(2)}, u32[]{:S(2)}) %collective-permute-start.1) | collective-permute-done | bytes 606240 | tf_op jit(solution)/shard_map/ppermute | solution.py:456
  45.4 3.2 %collective-permute-done.x.refs_1_ = bf16[296,1024]{1,0:T(8,128)(2,1)S(1)} collective-permute-done((bf16[296,1024]{1,0:T(8,128)(2,1)S(1)}, bf16[296,1024]{1,0:T(8,128)(2,1)S(1)}, u32[]{:S(2)}, u32[]{:S(2)}) %collective-permute-start) | collective-permute-done | bytes 606240 | tf_op jit(solution)/shard_map/ppermute | solution.py:455
  48.6 2.7 %collective-permute-start.3 = (bf16[296,1024]{1,0:T(8,128)(2,1)S(1)}, bf16[296,1024]{1,0:T(8,128)(2,1)S(1)}, u32[]{:S(2)}, u32[]{:S(2)}) collective-permute-start(bf16[296,1024]{1,0:T(8,128)(2,1)S(1)} %collective-permute-done.1.x.refs_2_), channel_id=1, source_target_pairs={{0,224},{32,0},{64,32},{96,64},{128,96},{160,128},{192,160},{224,1... | collective-permute-start | bytes 1818632 | tf_op jit(solution)/shard_map/ppermute | solution.py:456
  51.3 1.7 expert_forward.8
  54.3 1.7 expert_forward.9
  58.0 6.1 %collective-permute-done.2.x.refs_3_ = bf16[296,1024]{1,0:T(8,128)(2,1)S(1)} collective-permute-done((bf16[296,1024]{1,0:T(8,128)(2,1)S(1)}, bf16[296,1024]{1,0:T(8,128)(2,1)S(1)}, u32[]{:S(2)}, u32[]{:S(2)}) %collective-permute-start.2) | collective-permute-done | bytes 606240 | tf_op jit(solution)/shard_map/ppermute | solution.py:455
  64.3 2.7 %collective-permute-start.5 = (bf16[296,1024]{1,0:T(8,128)(2,1)S(1)}, bf16[296,1024]{1,0:T(8,128)(2,1)S(1)}, u32[]{:S(2)}, u32[]{:S(2)}) collective-permute-start(bf16[296,1024]{1,0:T(8,128)(2,1)S(1)} %collective-permute-done.3.x.refs_4_), channel_id=1, source_target_pairs={{0,224},{32,0},{64,32},{96,64},{128,96},{160,128},{192,160},{224,1... | collective-permute-start | bytes 1818632 | tf_op jit(solution)/shard_map/ppermute | solution.py:456
  67.0 1.7 expert_forward.10
  70.0 1.7 expert_forward.11
  74.4 4.5 %collective-permute-done.4.x.refs_5_ = bf16[296,1024]{1,0:T(8,128)(2,1)S(1)} collective-permute-done((bf16[296,1024]{1,0:T(8,128)(2,1)S(1)}, bf16[296,1024]{1,0:T(8,128)(2,1)S(1)}, u32[]{:S(2)}, u32[]{:S(2)}) %collective-permute-start.4) | collective-permute-done | bytes 606240 | tf_op jit(solution)/shard_map/ppermute | solution.py:455
  79.8 2.3 collective-permute-start.7
  82.9 1.1 copy-done.3
  84.0 1.7 expert_forward.12
  87.8 1.7 expert_forward.13
  91.7 2.8 %expert_forward_join.1 = (bf16[288,512]{1,0:T(8,128)(2,1)S(1)}, bf16[288,512]{1,0:T(8,128)(2,1)S(1)}, f32[288,128]{1,0:T(8,128)S(1)}, bf16[64,512]{1,0:T(8,128)(2,1)S(1)}, bf16[296,1024]{1,0:T(8,128)(2,1)S(1)}) custom-call(bf16[144,1024]{1,0:T(8,128)(2,1)} %collective-permute-done.6.top, bf16[152,1024]{1,0:T(8,128)(2,1)} %collective-permute-done.7.low, ...), custom_call_target="tpu_custom_call" | custom-call | tf_op jit(solution)/shard_map/expert_forward_join/pallas_call | solution.py:50
  96.8 2.3 pooled_down.1
  99.9 23.3 %all_to_all.31.got = bf16[32,16,1024]{2,1,0:T(8,128)(2,1)S(1)} all-to-all(bf16[32,16,1024]{2,1,0:T(8,128)(2,1)S(1)} %bitcast.59), channel_id=1, replica_groups=mesh['dp'=8,'expert'=32] {'expert'}, dimensions={0} | all-to-all | bytes 2097152 | tf_op jit(solution)/shard_map/all_to_all | solution.py:422
  123.9 16.3 %all_to_all.32.got = bf16[8,16,1024]{2,1,0:T(8,128)(2,1)S(1)} all-to-all(bf16[8,16,1024]{2,1,0:T(8,128)(2,1)S(1)} %column.1), channel_id=1, replica_groups=mesh['dp'=8,'expert'=32] {'dp'}, dimensions={0} | all-to-all | bytes 524288 | tf_op jit(solution)/shard_map/all_to_all | solution.py:422
  140.2 1.1 share.1
  141.3 4.8 %all-to-all-start.3 = ((bf16[32,16,1024]{2,1,0:T(8,128)(2,1)}), bf16[32,16,1024]{2,1,0:T(8,128)(2,1)}, u32[]{:S(2)}, u32[]{:S(2)}) async-start(bf16[32,16,1024]{2,1,0:T(8,128)(2,1)} %share.1), calls=%async_computation.3 | async-start | bytes 2097152 | tf_op jit(solution)/shard_map/all_to_all | solution.py:422
  147.4 15.8 %all-to-all-done.3.emb = bf16[32,16,1024]{2,1,0:T(8,128)(2,1)} async-done(((bf16[32,16,1024]{2,1,0:T(8,128)(2,1)}), bf16[32,16,1024]{2,1,0:T(8,128)(2,1)}, u32[]{:S(2)}, u32[]{:S(2)}) %all-to-all-start.3) | async-done | bytes 1048608 | tf_op jit(solution)/shard_map/all_to_all | solution.py:422
  163.2 4.2 %pair_loss.1 = (f32[1,1]{1,0:T(1,128)}, bf16[32,16,1024]{2,1,0:T(8,128)(2,1)S(1)}, f32[2,1024]{1,0:T(2,128)S(1)}, bf16[512,512]{1,0:T(8,128)(2,1)S(1)}) custom-call(s32[2]{0:T(128)S(1)} %pad_add_fusion.me, f32[1]{0:T(128)S(6)} %copy.16.scale, f32[1]{0:T(128)S(6)} %copy.17.bias, bf16[32,16,1024]{2,1,0:T(8,128)(2,1)} %all-to-all-done.3.emb, ...), custom_call_target="tpu_custom_call" | custom-call | tf_op jit(solution)/shard_map/pair_loss/pallas_call | solution.py:50
  167.5 1.7 expert_slope.8
  170.2 2.4 collective-permute-start.9
  172.6 1.8 expert_slope.15
  174.4 1.7 expert_slope.14
  176.2 1.7 expert_slope.13
  178.0 1.7 expert_slope.12
  179.8 1.7 expert_slope.11
  181.6 1.7 expert_slope.10
  183.4 1.7 expert_slope.9
  186.4 1.7 collective-permute-start.10
  188.2 7.7 %weight_grads.1 = (f32[1024,512]{1,0:T(8,128)}, f32[8,2,1024]{2,1,0:T(2,128)S(1)}) custom-call(bf16[296,1024]{1,0:T(8,128)(2,1)S(1)} %unpack.1.x.refs_0_, bf16[296,1024]{1,0:T(8,128)(2,1)S(1)} %copy-done.8, bf16[296,1024]{1,0:T(8,128)(2,1)S(1)} %copy-done.6, bf16[296,1024]{1,0:T(8,128)(2,1)S(1)} %copy-done.10, bf16[296,1024]{1,0:T(8,128)(2,1)S(1)} %copy-done.12, ...), custom_call_target="tpu_custom_call" | custom-call | tf_op jit(solution)/shard_map/weight_grads/pallas_call | solution.py:50
  195.9 4.1 %collective-permute-done.11.part = bf16[288,1024]{1,0:T(8,128)(2,1)S(1)} collective-permute-done((bf16[288,1024]{1,0:T(8,128)(2,1)S(1)}, bf16[288,1024]{1,0:T(8,128)(2,1)S(1)}, u32[]{:S(2)}, u32[]{:S(2)}) %collective-permute-start.11) | collective-permute-done | bytes 589856 | tf_op jit(solution)/shard_map/ppermute | solution.py:506
  200.0 2.0 collective-permute-done.10.part
  203.2 1.5 collective-permute-start.12
  204.7 14.3 %all_to_all.33.small = f32[8,2,1024]{2,1,0:T(2,128)S(1)} all-to-all(f32[8,2,1024]{2,1,0:T(2,128)S(1)} %get-tuple-element.235), channel_id=1, replica_groups=mesh['dp'=8,'expert'=32] {'dp'}, dimensions={0} | all-to-all | bytes 131072 | tf_op jit(solution)/shard_map/all_to_all | solution.py:422
  220.4 1.2 collective-permute-start.14
  222.2 10.2 %collective-permute-done.15.l = bf16[288,1024]{1,0:T(8,128)(2,1)S(1)} collective-permute-done((bf16[288,1024]{1,0:T(8,128)(2,1)S(1)}, bf16[288,1024]{1,0:T(8,128)(2,1)S(1)}, u32[]{:S(2)}, u32[]{:S(2)}) %collective-permute-start.15) | collective-permute-done | bytes 589856 | tf_op jit(solution)/shard_map/ppermute | solution.py:506
  232.9 1.5 back_last.1
  234.4 8.6 %all-to-all-start.5 = ((bf16[32,8,1408]{2,1,0:T(8,128)(2,1)}), bf16[32,8,1408]{2,1,0:T(8,128)(2,1)S(1)}, u32[]{:S(2)}, u32[]{:S(2)}) async-start(bf16[32,8,1408]{2,1,0:T(8,128)(2,1)} %bitcast.12), calls=%async_computation.5 | async-start | bytes 1441792 | tf_op jit(solution)/shard_map/all_to_all | solution.py:422
  243.1 2.1 down_grad.1
  245.2 11.5 %all-to-all-done.5 = bf16[32,8,1408]{2,1,0:T(8,128)(2,1)S(1)} async-done(((bf16[32,8,1408]{2,1,0:T(8,128)(2,1)}), bf16[32,8,1408]{2,1,0:T(8,128)(2,1)S(1)}, u32[]{:S(2)}, u32[]{:S(2)}) %all-to-all-start.5) | async-done | bytes 720928 | tf_op jit(solution)/shard_map/all_to_all | solution.py:422
  256.6 1.9 final.1
  (193 shorter events, 26.3 us)
Async XLA Ops:
  0.6 31.6 %copy-start = (bf16[1,1024,512]{2,1,0:T(8,128)(2,1)S(1)}, bf16[1,1024,512]{2,1,0:T(8,128)(2,1)}, u32[]{:S(2)}) copy-start(bf16[1,1024,512]{2,1,0:T(8,128)(2,1)} %param.14) | copy-start | bytes 3145732
  3.8 28.4 %copy-start.80 = (f32[1024,32]{0,1:T(8,128)S(1)}, f32[1024,32]{0,1:T(8,128)}, u32[]{:S(2)}) copy-start(f32[1024,32]{0,1:T(8,128)} %param.13) | copy-start | bytes 393220
  26.5 18.9 %collective-permute-start.1 = (bf16[296,1024]{1,0:T(8,128)(2,1)S(1)}, bf16[296,1024]{1,0:T(8,128)(2,1)S(1)}, u32[]{:S(2)}, u32[]{:S(2)}) collective-permute-start(bf16[296,1024]{1,0:T(8,128)(2,1)S(1)} %unpack.1.x.refs_0_), channel_id=1, source_target_pairs={{0,224},{32,0},{64,32},{96,64},{128,96},{160,128},{192,160},{224,1... | collective-permute-start | bytes 1818632 | tf_op jit(solution)/shard_map/ppermute | solution.py:456
  32.2 16.5 %collective-permute-start = (bf16[296,1024]{1,0:T(8,128)(2,1)S(1)}, bf16[296,1024]{1,0:T(8,128)(2,1)S(1)}, u32[]{:S(2)}, u32[]{:S(2)}) collective-permute-start(bf16[296,1024]{1,0:T(8,128)(2,1)S(1)} %unpack.1.x.refs_0_), channel_id=1, source_target_pairs={{0,32},{32,64},{64,96},{96,128},{128,160},{160,192},{192,224},{224... | collective-permute-start | bytes 1818632 | tf_op jit(solution)/shard_map/ppermute | solution.py:455
  34.7 29.5 %copy-start.21 = (bf16[288,512]{1,0:T(8,128)(2,1)}, bf16[288,512]{1,0:T(8,128)(2,1)S(1)}, u32[]{:S(2)}) copy-start(bf16[288,512]{1,0:T(8,128)(2,1)S(1)} %get-tuple-element.188.act) | copy-start | bytes 884740
  34.7 29.5 %copy-start.53 = (f32[288,128]{1,0:T(8,128)}, f32[288,128]{1,0:T(8,128)S(1)}, u32[]{:S(2)}) copy-start(f32[288,128]{1,0:T(8,128)S(1)} %get-tuple-element.190.cols) | copy-start | bytes 442372
  45.4 18.8 %copy-start.5 = (bf16[296,1024]{1,0:T(8,128)(2,1)}, bf16[296,1024]{1,0:T(8,128)(2,1)S(1)}, u32[]{:S(2)}) copy-start(bf16[296,1024]{1,0:T(8,128)(2,1)S(1)} %collective-permute-done.1.x.refs_2_) | copy-start | bytes 1818628
  48.6 15.6 %copy-start.7 = (bf16[296,1024]{1,0:T(8,128)(2,1)}, bf16[296,1024]{1,0:T(8,128)(2,1)S(1)}, u32[]{:S(2)}) copy-start(bf16[296,1024]{1,0:T(8,128)(2,1)S(1)} %collective-permute-done.x.refs_1_) | copy-start | bytes 1818628
  48.6 15.5 %collective-permute-start.2 = (bf16[296,1024]{1,0:T(8,128)(2,1)S(1)}, bf16[296,1024]{1,0:T(8,128)(2,1)S(1)}, u32[]{:S(2)}, u32[]{:S(2)}) collective-permute-start(bf16[296,1024]{1,0:T(8,128)(2,1)S(1)} %collective-permute-done.x.refs_1_), channel_id=1, source_target_pairs={{0,32},{32,64},{64,96},{96,128},{128,160},{160,192},{192,224},{224... | collective-permute-start | bytes 1818632 | tf_op jit(solution)/shard_map/ppermute | solution.py:455
  48.6 15.5 %collective-permute-start.3 = (bf16[296,1024]{1,0:T(8,128)(2,1)S(1)}, bf16[296,1024]{1,0:T(8,128)(2,1)S(1)}, u32[]{:S(2)}, u32[]{:S(2)}) collective-permute-start(bf16[296,1024]{1,0:T(8,128)(2,1)S(1)} %collective-permute-done.1.x.refs_2_), channel_id=1, source_target_pairs={{0,224},{32,0},{64,32},{96,64},{128,96},{160,128},{192,160},{224,1... | collective-permute-start | bytes 1818632 | tf_op jit(solution)/shard_map/ppermute | solution.py:456
  54.3 17.4 %copy-start.25 = (bf16[288,512]{1,0:T(8,128)(2,1)}, bf16[288,512]{1,0:T(8,128)(2,1)S(1)}, u32[]{:S(2)}) copy-start(bf16[288,512]{1,0:T(8,128)(2,1)S(1)} %get-tuple-element.183.act) | copy-start | bytes 884740
  54.3 17.4 %copy-start.27 = (bf16[288,512]{1,0:T(8,128)(2,1)}, bf16[288,512]{1,0:T(8,128)(2,1)S(1)}, u32[]{:S(2)}) copy-start(bf16[288,512]{1,0:T(8,128)(2,1)S(1)} %get-tuple-element.184.slope) | copy-start | bytes 884740
  58.0 20.9 %copy-start.29 = (bf16[288,512]{1,0:T(8,128)(2,1)}, bf16[288,512]{1,0:T(8,128)(2,1)S(1)}, u32[]{:S(2)}) copy-start(bf16[288,512]{1,0:T(8,128)(2,1)S(1)} %get-tuple-element.193.act) | copy-start | bytes 884740
  64.2 14.7 %copy-start.9 = (bf16[296,1024]{1,0:T(8,128)(2,1)}, bf16[296,1024]{1,0:T(8,128)(2,1)S(1)}, u32[]{:S(2)}) copy-start(bf16[296,1024]{1,0:T(8,128)(2,1)S(1)} %collective-permute-done.2.x.refs_3_) | copy-start | bytes 1818628
  64.2 14.7 %copy-start.11 = (bf16[296,1024]{1,0:T(8,128)(2,1)}, bf16[296,1024]{1,0:T(8,128)(2,1)S(1)}, u32[]{:S(2)}) copy-start(bf16[296,1024]{1,0:T(8,128)(2,1)S(1)} %collective-permute-done.3.x.refs_4_) | copy-start | bytes 1818628
  64.2 14.7 %collective-permute-start.4 = (bf16[296,1024]{1,0:T(8,128)(2,1)S(1)}, bf16[296,1024]{1,0:T(8,128)(2,1)S(1)}, u32[]{:S(2)}, u32[]{:S(2)}) collective-permute-start(bf16[296,1024]{1,0:T(8,128)(2,1)S(1)} %collective-permute-done.2.x.refs_3_), channel_id=1, source_target_pairs={{0,32},{32,64},{64,96},{96,128},{128,160},{160,192},{192,224},{224... | collective-permute-start | bytes 1818632 | tf_op jit(solution)/shard_map/ppermute | solution.py:455
  64.3 14.6 %collective-permute-start.5 = (bf16[296,1024]{1,0:T(8,128)(2,1)S(1)}, bf16[296,1024]{1,0:T(8,128)(2,1)S(1)}, u32[]{:S(2)}, u32[]{:S(2)}) collective-permute-start(bf16[296,1024]{1,0:T(8,128)(2,1)S(1)} %collective-permute-done.3.x.refs_4_), channel_id=1, source_target_pairs={{0,224},{32,0},{64,32},{96,64},{128,96},{160,128},{192,160},{224,1... | collective-permute-start | bytes 1818632 | tf_op jit(solution)/shard_map/ppermute | solution.py:456
  70.0 12.8 %copy-start.33 = (bf16[288,512]{1,0:T(8,128)(2,1)}, bf16[288,512]{1,0:T(8,128)(2,1)S(1)}, u32[]{:S(2)}) copy-start(bf16[288,512]{1,0:T(8,128)(2,1)S(1)} %get-tuple-element.178.act) | copy-start | bytes 884740
  70.0 12.8 %copy-start.59 = (f32[288,128]{1,0:T(8,128)}, f32[288,128]{1,0:T(8,128)S(1)}, u32[]{:S(2)}) copy-start(f32[288,128]{1,0:T(8,128)S(1)} %get-tuple-element.180.cols) | copy-start | bytes 442372
  79.8 11.9 %collective-permute-start.7 = (bf16[152,1024]{1,0:T(8,128)(2,1)}, bf16[152,1024]{1,0:T(8,128)(2,1)}, u32[]{:S(2)}, u32[]{:S(2)}) collective-permute-start(bf16[152,1024]{1,0:T(8,128)(2,1)} %slice.7), channel_id=1, source_target_pairs={{0,224},{32,0},{64,32},{96,64},{128,96},{160,128},{192,160},{224,1... | collective-permute-start | bytes 933896 | tf_op jit(solution)/shard_map/ppermute | solution.py:465
  82.8 8.9 %collective-permute-start.6 = (bf16[144,1024]{1,0:T(8,128)(2,1)}, bf16[144,1024]{1,0:T(8,128)(2,1)}, u32[]{:S(2)}, u32[]{:S(2)}) collective-permute-start(bf16[144,1024]{1,0:T(8,128)(2,1)} %slice.6), channel_id=1, source_target_pairs={{0,32},{32,64},{64,96},{96,128},{128,160},{160,192},{192,224},{224... | collective-permute-start | bytes 884744 | tf_op jit(solution)/shard_map/ppermute | solution.py:464
  83.9 12.8 %copy-start.1 = (bf16[1,512,1024]{2,1,0:T(8,128)(2,1)S(1)}, bf16[1,512,1024]{2,1,0:T(8,128)(2,1)}, u32[]{:S(2)}) copy-start(bf16[1,512,1024]{2,1,0:T(8,128)(2,1)} %param.15) | copy-start | bytes 3145732
  83.9 12.8 %copy-start.70 = (bf16[64,512]{1,0:T(8,128)(2,1)S(1)}, bf16[64,512]{1,0:T(8,128)(2,1)}, u32[]{:S(2)}) copy-start(bf16[64,512]{1,0:T(8,128)(2,1)} %copy-done.69) | copy-start | bytes 196612
  84.0 12.8 %copy-start.72 = (bf16[64,512]{1,0:T(8,128)(2,1)S(1)}, bf16[64,512]{1,0:T(8,128)(2,1)}, u32[]{:S(2)}) copy-start(bf16[64,512]{1,0:T(8,128)(2,1)} %copy-done.71) | copy-start | bytes 196612
  84.0 12.8 %copy-start.74 = (bf16[64,512]{1,0:T(8,128)(2,1)S(1)}, bf16[64,512]{1,0:T(8,128)(2,1)}, u32[]{:S(2)}) copy-start(bf16[64,512]{1,0:T(8,128)(2,1)} %copy-done.73) | copy-start | bytes 196612
  84.0 12.8 %copy-start.76 = (bf16[64,512]{1,0:T(8,128)(2,1)S(1)}, bf16[64,512]{1,0:T(8,128)(2,1)}, u32[]{:S(2)}) copy-start(bf16[64,512]{1,0:T(8,128)(2,1)} %copy-done.75) | copy-start | bytes 196612
  96.7 27.1 %copy-start.67 = (f32[288,128]{1,0:T(8,128)}, f32[288,128]{1,0:T(8,128)S(1)}, u32[]{:S(2)}) copy-start(f32[288,128]{1,0:T(8,128)S(1)} %get-tuple-element.168.cols) | copy-start | bytes 442372
  141.3 21.9 %all-to-all-start.3 = ((bf16[32,16,1024]{2,1,0:T(8,128)(2,1)}), bf16[32,16,1024]{2,1,0:T(8,128)(2,1)}, u32[]{:S(2)}, u32[]{:S(2)}) async-start(bf16[32,16,1024]{2,1,0:T(8,128)(2,1)} %share.1), calls=%async_computation.3 | async-start | bytes 2097152 | tf_op jit(solution)/shard_map/all_to_all | solution.py:422
  163.2 9.4 %copy-start.46 = (bf16[288,512]{1,0:T(8,128)(2,1)S(1)}, bf16[288,512]{1,0:T(8,128)(2,1)}, u32[]{:S(2)}) copy-start(bf16[288,512]{1,0:T(8,128)(2,1)} %copy-done.45) | copy-start | bytes 884740
  163.2 9.4 %copy-start.48 = (bf16[288,512]{1,0:T(8,128)(2,1)S(1)}, bf16[288,512]{1,0:T(8,128)(2,1)}, u32[]{:S(2)}) copy-start(bf16[288,512]{1,0:T(8,128)(2,1)} %copy-done.47) | copy-start | bytes 884740
  163.2 9.4 %copy-start.66 = (f32[288,128]{1,0:T(8,128)S(1)}, f32[288,128]{1,0:T(8,128)}, u32[]{:S(2)}) copy-start(f32[288,128]{1,0:T(8,128)} %copy-done.65) | copy-start | bytes 442372
  167.4 8.8 %copy-start.15 = (bf16[32,16,1024]{2,1,0:T(8,128)(2,1)}, bf16[32,16,1024]{2,1,0:T(8,128)(2,1)S(1)}, u32[]{:S(2)}) copy-start(bf16[32,16,1024]{2,1,0:T(8,128)(2,1)S(1)} %get-tuple-element.243.d_emb) | copy-start | bytes 3145732
  169.8 8.2 %copy-start.22 = (bf16[288,512]{1,0:T(8,128)(2,1)S(1)}, bf16[288,512]{1,0:T(8,128)(2,1)}, u32[]{:S(2)}) copy-start(bf16[288,512]{1,0:T(8,128)(2,1)} %copy-done.21) | copy-start | bytes 884740
  169.8 8.2 %copy-start.24 = (bf16[288,512]{1,0:T(8,128)(2,1)S(1)}, bf16[288,512]{1,0:T(8,128)(2,1)}, u32[]{:S(2)}) copy-start(bf16[288,512]{1,0:T(8,128)(2,1)} %copy-done.23) | copy-start | bytes 884740
  169.8 8.2 %copy-start.54 = (f32[288,128]{1,0:T(8,128)S(1)}, f32[288,128]{1,0:T(8,128)}, u32[]{:S(2)}) copy-start(f32[288,128]{1,0:T(8,128)} %copy-done.53) | copy-start | bytes 442372
  169.8 15.3 %collective-permute-start.8 = (bf16[144,1024]{1,0:T(8,128)(2,1)S(1)}, bf16[144,1024]{1,0:T(8,128)(2,1)S(1)}, u32[]{:S(2)}, u32[]{:S(2)}) collective-permute-start(bf16[144,1024]{1,0:T(8,128)(2,1)S(1)} %get-tuple-element.171), channel_id=1, source_target_pairs={{0,32},{32,64},{64,96},{96,128},{128,160},{160,192},{192,224},{224... | collective-permute-start | bytes 884744 | tf_op jit(solution)/shard_map/ppermute | solution.py:505
  170.2 15.0 %collective-permute-start.9 = (bf16[144,1024]{1,0:T(8,128)(2,1)S(1)}, bf16[144,1024]{1,0:T(8,128)(2,1)S(1)}, u32[]{:S(2)}, u32[]{:S(2)}) collective-permute-start(bf16[144,1024]{1,0:T(8,128)(2,1)S(1)} %get-tuple-element.172), channel_id=1, source_target_pairs={{0,224},{32,0},{64,32},{96,64},{128,96},{160,128},{192,160},{224,1... | collective-permute-start | bytes 884744 | tf_op jit(solution)/shard_map/ppermute | solution.py:506
  185.8 14.2 %collective-permute-start.11 = (bf16[288,1024]{1,0:T(8,128)(2,1)S(1)}, bf16[288,1024]{1,0:T(8,128)(2,1)S(1)}, u32[]{:S(2)}, u32[]{:S(2)}) collective-permute-start(bf16[288,1024]{1,0:T(8,128)(2,1)S(1)} %back_half.3), channel_id=1, source_target_pairs={{0,224},{32,0},{64,32},{96,64},{128,96},{160,128},{192,160},{224,1... | collective-permute-start | bytes 1769480 | tf_op jit(solution)/shard_map/ppermute | solution.py:506
  186.4 15.7 %collective-permute-start.10 = (bf16[288,1024]{1,0:T(8,128)(2,1)S(1)}, bf16[288,1024]{1,0:T(8,128)(2,1)S(1)}, u32[]{:S(2)}, u32[]{:S(2)}) collective-permute-start(bf16[288,1024]{1,0:T(8,128)(2,1)S(1)} %back_half.2), channel_id=1, source_target_pairs={{0,32},{32,64},{64,96},{96,128},{128,160},{160,192},{192,224},{224... | collective-permute-start | bytes 1769480 | tf_op jit(solution)/shard_map/ppermute | solution.py:505
  203.1 15.9 %collective-permute-start.13 = (bf16[288,1024]{1,0:T(8,128)(2,1)S(1)}, bf16[288,1024]{1,0:T(8,128)(2,1)S(1)}, u32[]{:S(2)}, u32[]{:S(2)}) collective-permute-start(bf16[288,1024]{1,0:T(8,128)(2,1)S(1)} %back.5), channel_id=1, source_target_pairs={{0,224},{32,0},{64,32},{96,64},{128,96},{160,128},{192,160},{224,1... | collective-permute-start | bytes 1769480 | tf_op jit(solution)/shard_map/ppermute | solution.py:506
  203.2 15.8 %collective-permute-start.12 = (bf16[288,1024]{1,0:T(8,128)(2,1)S(1)}, bf16[288,1024]{1,0:T(8,128)(2,1)S(1)}, u32[]{:S(2)}, u32[]{:S(2)}) collective-permute-start(bf16[288,1024]{1,0:T(8,128)(2,1)S(1)} %back.4), channel_id=1, source_target_pairs={{0,32},{32,64},{64,96},{96,128},{128,160},{160,192},{192,224},{224... | collective-permute-start | bytes 1769480 | tf_op jit(solution)/shard_map/ppermute | solution.py:505
  220.1 12.3 %collective-permute-start.15 = (bf16[288,1024]{1,0:T(8,128)(2,1)S(1)}, bf16[288,1024]{1,0:T(8,128)(2,1)S(1)}, u32[]{:S(2)}, u32[]{:S(2)}) collective-permute-start(bf16[288,1024]{1,0:T(8,128)(2,1)S(1)} %back.7), channel_id=1, source_target_pairs={{0,224},{32,0},{64,32},{96,64},{128,96},{160,128},{192,160},{224,1... | collective-permute-start | bytes 1769480 | tf_op jit(solution)/shard_map/ppermute | solution.py:506
  220.4 12.4 %collective-permute-start.14 = (bf16[288,1024]{1,0:T(8,128)(2,1)S(1)}, bf16[288,1024]{1,0:T(8,128)(2,1)S(1)}, u32[]{:S(2)}, u32[]{:S(2)}) collective-permute-start(bf16[288,1024]{1,0:T(8,128)(2,1)S(1)} %back.6), channel_id=1, source_target_pairs={{0,32},{32,64},{64,96},{96,128},{128,160},{160,192},{192,224},{224... | collective-permute-start | bytes 1769480 | tf_op jit(solution)/shard_map/ppermute | solution.py:505
  222.2 20.9 %copy-start.16 = (bf16[32,16,1024]{2,1,0:T(8,128)(2,1)S(1)}, bf16[32,16,1024]{2,1,0:T(8,128)(2,1)}, u32[]{:S(2)}) copy-start(bf16[32,16,1024]{2,1,0:T(8,128)(2,1)} %copy-done.15) | copy-start | bytes 3145732
  222.2 20.9 %copy-start.20 = (bf16[512,512]{1,0:T(8,128)(2,1)S(1)}, bf16[512,512]{1,0:T(8,128)(2,1)}, u32[]{:S(2)}) copy-start(bf16[512,512]{1,0:T(8,128)(2,1)} %copy-done.19) | copy-start | bytes 1572868
  234.4 22.2 %all-to-all-start.5 = ((bf16[32,8,1408]{2,1,0:T(8,128)(2,1)}), bf16[32,8,1408]{2,1,0:T(8,128)(2,1)S(1)}, u32[]{:S(2)}, u32[]{:S(2)}) async-start(bf16[32,8,1408]{2,1,0:T(8,128)(2,1)} %bitcast.12), calls=%async_computation.5 | async-start | bytes 1441792 | tf_op jit(solution)/shard_map/all_to_all | solution.py:422
  243.0 13.6 %copy-start.14 = (bf16[1,212,1024]{2,1,0:T(8,128)(2,1)S(1)}, bf16[1,212,1024]{2,1,0:T(8,128)(2,1)}, u32[]{:S(2)}) copy-start(bf16[1,212,1024]{2,1,0:T(8,128)(2,1)} %param.9) | copy-start | bytes 1302532
  243.1 13.6 %copy-start.78 = (f32[1024]{0:T(1024)S(1)}, f32[1024]{0:T(1024)}, u32[]{:S(2)}) copy-start(f32[1024]{0:T(1024)} %param.12) | copy-start | bytes 12292
  (51 other events, 143.3 us)
